TPU v7x, 32 devices: a whole 2x2x4 slice. The times are simulated.
32 devices in a mesh: clip: 4 (over z), sp: 4 (over x, core), tp: 2 (over y).
Axes of the slice: x: 2, y: 2, z: 4, core: 2. Of those that a mesh axis runs over, the one named last changes fastest.
Arguments:
- latents: bfloat16 [4, 4, 1024, 512], P('clip', 'sp', None, 'tp'), may hold values from -6 to 6
- saved_input: bfloat16 [4, 4, 1024, 512], P('clip', None, 'sp', 'tp'), may hold values from -6 to 6
- out_grad: bfloat16 [4, 4, 1024, 512], P('clip', None, 'sp', 'tp'), may hold values from -6 to 6
- temporal_weight: bfloat16 [3, 512, 512], P(None, 'tp'), may hold values from -0.15625 to 0.15625
- spatial_weight: bfloat16 [9, 512, 512], P(None, 'tp'), may hold values from -0.09375 to 0.09375
Outputs:
- input_grad: bfloat16 [4, 4, 1024, 512], P('clip', 'sp', None, 'tp')
- temporal_grad: float32 [3, 512, 512], P(None, 'tp', 'sp')
- spatial_grad: float32 [9, 512, 512], P(None, 'tp', 'sp')
All inputs are finite; a program needn't handle non-finite values.
Results may differ from a plain program's by a relative error of at most 0.005.
Values may be sent and summed in bfloat16 or wider, within the bound.
A program may use at most 64 MiB of HBM per device.

v0:
```python
import functools
import math

import jax
import jax.numpy as jnp
from jax import lax
from jax.experimental import pallas as pl
from jax.experimental.pallas import tpu as pltpu
from jax.sharding import PartitionSpec as P

HS = 32
WS = 32
MESH = pl.DeviceIdType.MESH
F32 = jnp.float32
BF16 = jnp.bfloat16


def pad_frames(values):
    return jnp.pad(values, ((0, 0), (1, 1), (0, 0), (0, 0)))


def nt(a, b):
    return lax.dot_general(a, b, (((1,), (1,)), ((), ())), preferred_element_type=F32)


def nn(a, b):
    return lax.dot_general(a, b, (((1,), (0,)), ((), ())), preferred_element_type=F32)


def chunks_of(taps, size):
    return [(start, min(size, taps - start)) for start in range(0, taps, size)]


def order(chunks, first, images, tap_kb):
    hop, rate = 2.5, 40.0
    now, free = 0.0, {"core": 0.0, "x": 0.0, "z": 0.0, "back": 0.0}
    pending, out = {}, []

    def send(link, n, step):
        cost = chunks[n][1] * tap_kb / rate if link != "core" else chunks[n][1] * tap_kb / 100.0
        free[link] = max(free[link], now) + cost
        pending[step, n] = free[link] + hop

    for n in range(first):
        send("z", n, 3)
    grads, filler = list(range(first, len(chunks))), list(range(images))
    while pending or grads or filler:
        ready = sorted((at, key) for key, at in pending.items() if at <= now)
        if grads and (not ready or len(ready) < 2):
            n = grads.pop(0)
            out.append(("g", n))
            now += 0.8 * chunks[n][1]
            send("core", n, 1)
        elif ready or not filler:
            at, (step, n) = ready[0] if ready else min((at, key) for key, at in pending.items())
            now = max(now, at) + 0.12 * chunks[n][1]
            del pending[step, n]
            out.append((step, n))
            if step == 1:
                send("x", n, 2)
            elif step == 2:
                send("z", n, 3)
            elif step == 3:
                send("z", n, 4)
            elif step == 4:
                send("back", n, 5)
        else:
            n = filler.pop(0)
            out.append(("i", n))
            now += 0.7
    return out


def kernel(
    dims, lat, sav, og, tw, sw, ig, gf,
    latv, savv, twv, swv, opad, hsend, hrecv, hwide, hs, savt, latt, acc,
    gsend, g1, g2s, g2r, gz, gzf, gzr,
    lsem, osend, orecv, osem, hsendsem, hrecvsem, hlocsem,
    s1s, s1r, s2s, s2r, s3s, s3r,
):
    S, T, Z, F, Pl, Cl, Cs, scale, chunks, KT = dims
    U = S // 2
    HW = S * Pl
    C = T * Cl
    me_s, me_t, me_z = lax.axis_index("sp"), lax.axis_index("tp"), lax.axis_index("clip")
    me_u, me_c = me_s // 2, lax.rem(me_s, 2)

    loads = [
        pltpu.make_async_copy(src, dst, lsem.at[n])
        for n, (src, dst) in enumerate(((sav, savv), (tw, twv), (lat, latv), (sw, swv)))
    ]
    for copy in loads:
        copy.start()
    my_cols = pl.ds(pl.multiple_of(me_t * Cl, Cl), Cl)
    mine = [
        pltpu.make_async_copy(og.at[pl.ds(f * Pl, Pl)], opad.at[pl.ds((f + 1) * Pl, Pl), my_cols], osem.at[f])
        for f in range(F)
    ]
    for copy in mine:
        copy.start()

    barrier = pltpu.get_barrier_semaphore()
    count = 0
    for ds_ in range(S):
        for dt in range(T):
            if ds_ == 0 and dt == 0:
                continue
            count += 1
            pl.semaphore_signal(
                barrier, inc=1, device_id=(me_z, lax.rem(me_s + ds_, S), lax.rem(me_t + dt, T)),
                device_id_type=MESH,
            )
    for dz in range(1, Z):
        count += 1
        pl.semaphore_signal(
            barrier, inc=1, device_id=(lax.rem(me_z + dz, Z), me_s, me_t), device_id_type=MESH
        )
    pl.semaphore_wait(barrier, count)

    ocopies = []
    for d in range(F):
        f = lax.rem(me_s + d, F)
        ocopies.append([])
        for dt in range(1, T):
            copy = pltpu.make_async_remote_copy(
                src_ref=og.at[pl.ds(pl.multiple_of(f * Pl, Pl), Pl)],
                dst_ref=opad.at[pl.ds(pl.multiple_of((f + 1) * Pl, Pl), Pl), my_cols],
                send_sem=osend.at[d, dt - 1], recv_sem=orecv.at[d, dt - 1],
                device_id=(me_z, me_s, lax.rem(me_t + dt, T)), device_id_type=MESH,
            )
            copy.start()
            ocopies[-1].append(copy)

    opad[pl.ds(0, Pl), :] = jnp.zeros((Pl, C), BF16)
    opad[pl.ds((F + 1) * Pl, Pl), :] = jnp.zeros((Pl, C), BF16)
    hwide[pl.ds(0, 8), :] = jnp.zeros((8, C), F32)
    hwide[pl.ds(8 + HW, 8), :] = jnp.zeros((8, C), F32)
    for b in range(3):
        hs[b, pl.ds(0, WS), :] = jnp.zeros((WS, C), BF16)
        hs[b, pl.ds(WS + HW, WS), :] = jnp.zeros((WS, C), BF16)
    loads[0].wait()
    savt[...] = savv[...].T
    loads[2].wait()
    latt[...] = latv[...].T
    loads[1].wait()
    loads[3].wait()
    for copy in mine:
        copy.wait()
    arrived = set()

    hcopies = []
    for d in list(range(1, S)) + [0]:
        f = lax.rem(me_s + d, S)
        rows = pl.ds(pl.multiple_of(f * Pl, Pl), Pl)
        for need in range(d - 1, d + 2):
            if need % F not in arrived:
                arrived.add(need % F)
                for copy in ocopies[need % F]:
                    copy.wait()
        total = None
        for k in range(KT):
            moved = opad[pl.ds(pl.multiple_of((f + KT - 1 - k) * Pl, Pl), Pl), :]
            term = nt(moved, twv[k])
            total = term if total is None else total + term
        hsend[rows, :] = total.astype(BF16)
        dst = hrecv.at[pl.ds(pl.multiple_of(me_s * Pl, Pl), Pl), my_cols]
        for dt in range(T):
            if d == 0 and dt == 0:
                own = pltpu.make_async_copy(hsend.at[rows], dst, hlocsem)
                own.start()
                continue
            copy = pltpu.make_async_remote_copy(
                src_ref=hsend.at[rows], dst_ref=dst,
                send_sem=hsendsem.at[d, dt], recv_sem=hrecvsem.at[d, dt],
                device_id=(me_z, f, lax.rem(me_t + dt, T)), device_id_type=MESH,
            )
            copy.start()
            hcopies.append(copy)

    sent = {}

    def store_partial(tap, part):
        for s in range(S):
            gsend[s % 2, s // 2, tap] = part[:, s * Cs : (s + 1) * Cs].astype(BF16)

    def start1(n):
        at, size = chunks[n]
        copy = pltpu.make_async_remote_copy(
            src_ref=gsend.at[1 - me_c, :, pl.ds(at, size)], dst_ref=g1.at[:, pl.ds(at, size)],
            send_sem=s1s.at[n], recv_sem=s1r.at[n],
            device_id=(me_z, me_u * 2 + 1 - me_c, me_t), device_id_type=MESH,
        )
        copy.start()
        sent[1, n] = [copy]

    def step1(n):
        at, size = chunks[n]
        taps = pl.ds(at, size)
        for copy in sent[1, n]:
            copy.wait()
        g2s[:, taps] = (gsend[me_c, :, taps].astype(F32) + g1[:, taps].astype(F32)).astype(BF16)
        copies = []
        for d in range(1, U):
            other = lax.rem(me_u + d, U)
            copy = pltpu.make_async_remote_copy(
                src_ref=g2s.at[other, taps], dst_ref=g2r.at[d - 1, taps],
                send_sem=s2s.at[n, d - 1], recv_sem=s2r.at[n, d - 1],
                device_id=(me_z, other * 2 + me_c, me_t), device_id_type=MESH,
            )
            copy.start()
            copies.append(copy)
        sent[2, n] = copies

    def step2(n):
        at, size = chunks[n]
        taps = pl.ds(at, size)
        for copy in sent[2, n]:
            copy.wait()
        total = gsend[me_c, me_u, taps].astype(F32) + g1[me_u, taps].astype(F32)
        for d in range(1, U):
            total = total + g2r[d - 1, taps].astype(F32)
        gzf[taps] = total
        gz[taps] = total.astype(BF16)

        @pl.when(jnp.logical_and(is_end, jnp.logical_not(is_inner)))
        def _():
            to_inner(n).start()

    half = Z // 2
    low = me_z < half
    is_end = jnp.logical_or(me_z == 0, me_z == Z - 1)
    is_inner = jnp.logical_or(me_z == half - 1, me_z == half)
    z_in = jnp.where(low, me_z + 1, me_z - 1)
    z_out = jnp.clip(jnp.where(low, me_z - 1, me_z + 1), 0, Z - 1)
    Z_INNER, Z_OUTER = 0, 1

    def hop(n, src, slot, target):
        at, size = chunks[n]
        taps = pl.ds(at, size)
        return pltpu.make_async_remote_copy(
            src_ref=src.at[taps], dst_ref=gzr.at[slot, taps],
            send_sem=s3s.at[slot, n], recv_sem=s3r.at[slot, n],
            device_id=(target, me_s, me_t), device_id_type=MESH,
        )

    def to_inner(n):
        return hop(n, gz, Z_OUTER, z_in)

    def across(n):
        return hop(n, gz, Z_INNER, z_in)

    def to_outer(n):
        return hop(n, gf, Z_INNER, z_out)

    def step3(n):
        at, size = chunks[n]
        taps = pl.ds(at, size)

        @pl.when(jnp.logical_not(is_end))
        def _():
            to_inner(n).wait_recv()
            gz[taps] = (gzf[taps] + gzr[Z_OUTER, taps].astype(F32)).astype(BF16)

            @pl.when(jnp.logical_not(is_inner))
            def _():
                to_inner(n).start()

        @pl.when(is_inner)
        def _():
            across(n).start()

    def output(n):
        @pl.when(jnp.logical_not(is_end))
        def _():
            to_outer(n).start()

    def step4(n):
        at, size = chunks[n]
        taps = pl.ds(at, size)

        @pl.when(is_inner)
        def _():
            across(n).wait_recv()
            gf[taps] = (gz[taps].astype(F32) + gzr[Z_INNER, taps].astype(F32)).astype(BF16)
            output(n)

    def step5(n):
        at, size = chunks[n]
        taps = pl.ds(at, size)

        @pl.when(jnp.logical_not(is_inner))
        def _():
            across(n).wait_recv()
            gf[taps] = gzr[Z_INNER, taps]
            output(n)

    def finish(n):
        @pl.when(is_inner)
        def _():
            across(n).wait_send()

        @pl.when(jnp.logical_not(is_inner))
        def _():
            to_inner(n).wait_send()

        @pl.when(jnp.logical_not(is_end))
        def _():
            to_outer(n).wait_send()

    first = len([0 for at, _ in chunks if at < KT])
    for n in range(first):
        at, size = chunks[n]

        @pl.loop(at, at + size)
        def _(k):
            moved = opad[pl.ds(pl.multiple_of((KT - 1 - k) * Pl, Pl), F * Pl), :]
            store_partial(k, nn(savt[...], moved))

        start1(n)
    for n in range(first):
        step1(n)
    for n in range(first):
        step2(n)

    own.wait()
    for copy in hcopies:
        copy.wait()

    tile = 4 * WS
    for r in range(0, HW, tile):
        hwide[pl.ds(8 + r, tile), :] = hrecv[pl.ds(r, tile), :].astype(F32)
        hs[1, pl.ds(WS + r, tile), :] = hrecv[pl.ds(r, tile), :]
    column = lax.rem(lax.broadcasted_iota(jnp.int32, (tile, C), 0), WS)
    for b in (-1, 1):
        keep = column != (0 if b == 1 else WS - 1)
        for r in range(0, HW, tile):
            value = hwide[pl.ds(8 + r - b, tile), :]
            hs[b + 1, pl.ds(WS + r, tile), :] = jnp.where(keep, value, 0.0).astype(BF16)

    def moved_at(tap):
        row, col = tap // 3, lax.rem(tap, 3)
        return hs[col, pl.ds(pl.multiple_of((2 - row) * WS, WS), HW), :]

    def gradient(n):
        at, size = chunks[n]

        @pl.loop(at - KT, at - KT + size)
        def _(tap):
            store_partial(tap + KT, nn(latt[...], moved_at(tap)))

        start1(n)

    taps_left = swv.shape[0]

    def image(tap):
        term = nt(moved_at(tap), swv[tap])
        if tap == 0:
            acc[...] = term
        elif tap < taps_left - 1:
            acc[...] += term
        else:
            ig[...] = (acc[...] + term).astype(BF16)

    steps = {1: step1, 2: step2, 3: step3, 4: step4, 5: step5}
    total = len(chunks)
    for kind, n in order(chunks, first, taps_left, Cl * Cs * 2e-3):
        if kind == "g":
            gradient(n)
        elif kind == "i":
            image(n)
        else:
            steps[kind](n)
    for n in range(total):
        finish(n)


def fused(sizes, chunk, latents, saved_input, out_grad, temporal_weight, spatial_weight):
    S, T, Z = sizes
    F, Pl, Cl = out_grad.shape[1:]
    KT, _, C = temporal_weight.shape
    taps = KT + spatial_weight.shape[0]
    HW = latents.shape[2]
    Cs = C // S
    U = S // 2
    scale = 1.0 / math.sqrt(Z * F * HS * WS)
    chunks = chunks_of(KT, chunk) + [(KT + at, n) for at, n in chunks_of(taps - KT, chunk)]
    N = len(chunks)
    dims = (S, T, Z, F, Pl, Cl, Cs, scale, chunks, KT)
    V = pltpu.VMEM
    D = pltpu.SemaphoreType.DMA
    hbm = pl.BlockSpec(memory_space=pltpu.HBM)
    vmem = pl.BlockSpec(memory_space=pltpu.VMEM)
    ig, sums = pl.pallas_call(
        functools.partial(kernel, dims),
        out_shape=(
            jax.ShapeDtypeStruct((HW, Cl), BF16),
            jax.ShapeDtypeStruct((taps, Cl, Cs), BF16),
        ),
        in_specs=[hbm] * 5,
        out_specs=(vmem,) * 2,
        scratch_shapes=[
            V((HW, Cl), BF16), V((F * Pl, Cl), BF16), V((KT, Cl, C), BF16), V((taps - KT, Cl, C), BF16),
            V(((F + 2) * Pl, C), BF16), V((F * Pl, Cl), BF16), V((HW, C), BF16),
            V((HW + 16, C), F32), V((3, HW + 2 * WS, C), BF16),
            V((Cl, F * Pl), BF16), V((Cl, HW), BF16), V((HW, Cl), F32),
            V((2, U, taps, Cl, Cs), BF16), V((U, taps, Cl, Cs), BF16), V((U, taps, Cl, Cs), BF16),
            V((U - 1, taps, Cl, Cs), BF16), V((taps, Cl, Cs), BF16), V((taps, Cl, Cs), F32), V((2, taps, Cl, Cs), BF16),
            D((4,)), D((F, T - 1)), D((F, T - 1)), D((F,)), D((S, T)), D((S, T)), D(()),
            D((N,)), D((N,)), D((N, U - 1)), D((N, U - 1)),
            D((2, N)), D((2, N)),
        ],
        compiler_params=pltpu.CompilerParams(
            collective_id=0, has_side_effects=True, vmem_limit_bytes=63 * 2**20
        ),
    )(
        latents.reshape(HW, Cl), saved_input.reshape(F * Pl, Cl), out_grad.reshape(F * Pl, Cl),
        temporal_weight, spatial_weight,
    )

    def finish(ig_ref, sums_ref, ig_out, tg_out, sg_out):
        ig_out[...] = ig_ref[...]
        tg_out[...] = sums_ref[:KT].astype(F32) * scale
        sg_out[...] = sums_ref[KT:].astype(F32) * scale

    ig, tg, sg = pl.pallas_call(
        finish,
        out_shape=(
            jax.ShapeDtypeStruct((HW, Cl), BF16),
            jax.ShapeDtypeStruct((KT, Cl, Cs), F32),
            jax.ShapeDtypeStruct((taps - KT, Cl, Cs), F32),
        ),
        in_specs=[vmem] * 2,
        out_specs=(vmem,) * 3,
        compiler_params=pltpu.CompilerParams(vmem_limit_bytes=16 * 2**20),
    )(ig, sums)
    return ig.reshape(latents.shape), tg, sg


def plain(latents, saved_input, out_grad, temporal_weight, spatial_weight):
    clips_all = latents.shape[0] * lax.axis_size("clip")
    frames_all = latents.shape[1] * lax.axis_size("sp")
    scale_factor = 1.0 / math.sqrt(clips_all * frames_all * HS * WS)
    frames_count = out_grad.shape[1]
    local_in = temporal_weight.shape[1]
    saved_padded = pad_frames(saved_input)
    block_in = lax.all_gather(out_grad, "tp", axis=3, tiled=True)
    padded = pad_frames(block_in)
    hidden_acc = jnp.zeros(out_grad.shape[:3] + (local_in,), F32)
    parts = []
    for tap_index in range(3):
        shifted = padded[:, 2 - tap_index : 2 - tap_index + frames_count]
        hidden_acc = hidden_acc + jnp.einsum(
            "bfpo,io->bfpi", shifted, temporal_weight[tap_index], preferred_element_type=F32
        )
        window = saved_padded[:, tap_index : tap_index + frames_count]
        parts.append(jnp.einsum("bfpi,bfpo->io", window, block_in, preferred_element_type=F32))
    temporal_local = jnp.stack(parts)
    hidden_grad = hidden_acc.astype(BF16)
    regrouped = lax.all_to_all(hidden_grad, "sp", split_axis=1, concat_axis=2, tiled=True)
    batch = latents.shape[0] * latents.shape[1]
    image_pad = jnp.pad(latents.reshape(batch, HS, WS, local_in), ((0, 0), (1, 1), (1, 1), (0, 0)))
    block_in = lax.all_gather(regrouped, "tp", axis=3, tiled=True)
    whole = block_in.reshape(batch, HS, WS, block_in.shape[3])
    grid = jnp.pad(whole, ((0, 0), (1, 1), (1, 1), (0, 0)))
    input_acc = jnp.zeros((batch, HS, WS, local_in), F32)
    parts = []
    for row in (-1, 0, 1):
        for col in (-1, 0, 1):
            tap_index = 3 * (row + 1) + (col + 1)
            moved = grid[:, 1 - row : 1 - row + HS, 1 - col : 1 - col + WS]
            input_acc = input_acc + jnp.einsum(
                "gabo,co->gabc", moved, spatial_weight[tap_index], preferred_element_type=F32
            )
            window = image_pad[:, 1 + row : 1 + row + HS, 1 + col : 1 + col + WS]
            parts.append(jnp.einsum("gabc,gabo->co", window, whole, preferred_element_type=F32))
    spatial_local = jnp.stack(parts)
    input_grad = input_acc.reshape(latents.shape).astype(BF16)
    temporal_grad, spatial_grad = lax.psum(
        tuple(
            lax.psum_scatter(value * scale_factor, "sp", scatter_dimension=2, tiled=True)
            for value in (temporal_local, spatial_local)
        ),
        "clip",
    )
    return input_grad, temporal_grad, spatial_grad


CHUNK = 1


def solution(mesh):
    sizes = (mesh.shape["sp"], mesh.shape["tp"], mesh.shape["clip"])

    def local(latents, saved_input, out_grad, temporal_weight, spatial_weight):
        S, T, Z = sizes
        cols = temporal_weight.shape[2] // S
        fits = (
            latents.shape[:2] == (1, 1) and S % 2 == 0 and S > 2 and T > 1 and Z % 2 == 0
            and cols % 128 == 0 and out_grad.shape[3] % 128 == 0
        )
        args = (latents, saved_input, out_grad, temporal_weight, spatial_weight)
        return fused(sizes, CHUNK, *args) if fits else plain(*args)

    return jax.shard_map(
        local,
        mesh=mesh,
        in_specs=(
            P("clip", "sp", None, "tp"),
            P("clip", None, "sp", "tp"),
            P("clip", None, "sp", "tp"),
            P(None, "tp", None),
            P(None, "tp", None),
        ),
        out_specs=(P("clip", "sp", None, "tp"), P(None, "tp", "sp"), P(None, "tp", "sp")),
        check_vma=False,
    )
```

profile of v0, /device:TPU:0, one launch (start us, length us, event | category | flops | bytes accessed | tf_op | source)
XLA Modules:
  0.0 68.5 jit_solution(13062659758024847109)
XLA Ops:
  0.6 64.3 %shard_map.76 = (bf16[1024,256]{1,0:T(8,128)(2,1)}, bf16[12,256,128]{2,1,0:T(8,128)(2,1)}) custom-call(bf16[1024,256]{1,0:T(8,128)(2,1)} %bitcast.4, bf16[1024,256]{1,0:T(8,128)(2,1)} %bitcast.5, bf16[1024,256]{1,0:T(8,128)(2,1)} %bitcast.6, bf16[3,256,512]{2,1,0:T(8,128)(2,1)} %tw.1, bf16[9,256,512]{2,1,0:T(8,128)(2,1)} %sw.1), custom_call_target="tpu_custom_call" | custom-call | tf_op jit(solution)/shard_map/pallas_call | solution.py:393
  64.9 0.0 copy-start
  64.9 1.1 %copy-done = bf16[12,256,128]{2,1,0:T(8,128)(2,1)S(1)} copy-done((bf16[12,256,128]{2,1,0:T(8,128)(2,1)S(1)}, bf16[12,256,128]{2,1,0:T(8,128)(2,1)}, u32[]{:S(2)}) %copy-start) | copy-done | bytes 786456
  66.0 0.0 copy-start.1
  66.0 1.0 %copy-done.1 = bf16[1024,256]{1,0:T(8,128)(2,1)S(1)} copy-done((bf16[1024,256]{1,0:T(8,128)(2,1)S(1)}, bf16[1024,256]{1,0:T(8,128)(2,1)}, u32[]{:S(2)}) %copy-start.1) | copy-done | bytes 524312
  67.1 1.4 %shard_map.77 = (bf16[1024,256]{1,0:T(8,128)(2,1)}, f32[3,256,128]{2,1,0:T(8,128)}, f32[9,256,128]{2,1,0:T(8,128)}) custom-call(bf16[1024,256]{1,0:T(8,128)(2,1)S(1)} %copy-done.1, bf16[12,256,128]{2,1,0:T(8,128)(2,1)S(1)} %copy-done), custom_call_target="tpu_custom_call" | custom-call | tf_op jit(solution)/shard_map/pallas_call | solution.py:425
Async XLA Ops:
  64.9 1.1 %copy-start = (bf16[12,256,128]{2,1,0:T(8,128)(2,1)S(1)}, bf16[12,256,128]{2,1,0:T(8,128)(2,1)}, u32[]{:S(2)}) copy-start(bf16[12,256,128]{2,1,0:T(8,128)(2,1)} %get-tuple-element.9.sums_ref) | copy-start | bytes 2359300
  66.0 1.0 %copy-start.1 = (bf16[1024,256]{1,0:T(8,128)(2,1)S(1)}, bf16[1024,256]{1,0:T(8,128)(2,1)}, u32[]{:S(2)}) copy-start(bf16[1024,256]{1,0:T(8,128)(2,1)} %get-tuple-element.8.ig_ref) | copy-start | bytes 1572868
where the time goes:
time: 68.7 us; the launch traced here: 68.5 us
  Pallas kernels  65.7 us (96%)
  local copies, waits for them, and re-layouts  2.17 us (3%)
    pallas_call x1, Pallas kernels, fused(): pl.pallas_call(functools.partial(kernel, dims), out_shape=(jax.ShapeDtype...  64.3 us
    unnamed x4, local copies, waits for them, and re-layouts  2.17 us
    pallas_call x1, Pallas kernels, fused(): pl.pallas_call(finish, out_shape=(jax.ShapeDtypeStruct((HW, Cl), BF16), j...  1.4 us

commit v1 on v0

v1 whole, which is shorter than its diff:
```python
import contextlib
import functools
import math

import jax
import jax.numpy as jnp
from jax import lax
from jax.experimental import pallas as pl
from jax.experimental.pallas import tpu as pltpu
from jax.sharding import PartitionSpec as P

HS = 32
WS = 32
MESH = pl.DeviceIdType.MESH
F32 = jnp.float32
BF16 = jnp.bfloat16


def pad_frames(values):
    return jnp.pad(values, ((0, 0), (1, 1), (0, 0), (0, 0)))


def nt(a, b):
    return lax.dot_general(a, b, (((1,), (1,)), ((), ())), preferred_element_type=F32)


def nn(a, b):
    return lax.dot_general(a, b, (((1,), (0,)), ((), ())), preferred_element_type=F32)


scope = contextlib.nullcontext


def pieces_of(taps, parts, rows):
    return [(tap, part * (rows // n), rows // n) for tap, n in zip(taps, parts) for part in range(n)]


def order(chunks, first, images, rows):
    hop, core_hop, link, core = 1.8, 0.7, 1.39, 0.44
    arrival = 9.5
    now, free = 0.0, {"core": 0.0, "x": 2.0, "z": 0.0, "across": 0.0, "back": 0.0}
    pending, out = {}, []

    def send(name, n, step):
        part = chunks[n][2] / rows
        free[name] = max(free[name], now) + (core if name == "core" else link) * part
        pending[step, n] = free[name] + (core_hop if name == "core" else hop)

    taps = list(dict.fromkeys(tap for tap, _, _ in chunks))
    early, late, filler = taps[:first], taps[first:], list(range(images))
    shifted = False
    started = False
    while pending or early or late or filler:
        ready = sorted((at, key) for key, at in pending.items() if at <= now)
        if ready:
            at, (step, n) = ready[0]
            now += 0.08 * chunks[n][2] / rows
            del pending[step, n]
            out.append((step, n))
            if step < 5:
                send(("core", "x", "z", "across", "back")[step], n, step + 1)
            continue
        if not started and not early and now >= arrival:
            started = True
            out.append(("h", 0))
            continue
        soon = min(pending.values()) if pending else 1e9
        if not started and not early:
            soon = min(soon, arrival)
        if early or (started and late):
            if started and not shifted and len(taps) - first - len(late) >= 3:
                shifted = True
                out.append(("s", 0))
                now += 0.5
                continue
            tap = (early or late).pop(0)
            out.append(("g", tap))
            now += 0.45
            for n, chunk in enumerate(chunks):
                if chunk[0] == tap:
                    send("core", n, 1)
        elif started and filler and (soon > now + 0.3 or not pending):
            out.append(("i", filler.pop(0)))
            now += 0.58
        else:
            now = max(now, soon)
    return out


def kernel(
    dims, lat, sav, og, tw, sw, ig, gf,
    latv, savv, twv, swv, opad, hsend, hwide, hs, savt, latt, acc,
    gsend, g1, g2s, g2r, gz, gzf, gzr,
    lsem, osend, orecv, osem, xsend, xrecv, bsend, brecv, ysend, yrecv,
    s1s, s1r, s2s, s2r, s3s, s3r,
):
    S, T, Z, F, Pl, Cl, Cs, chunks, KT = dims
    U = S // 2
    HW = S * Pl
    C = T * Cl
    me_s, me_t, me_z = lax.axis_index("sp"), lax.axis_index("tp"), lax.axis_index("clip")
    me_u, me_c = me_s // 2, lax.rem(me_s, 2)
    sib = me_u * 2 + 1 - me_c
    far = (1 - me_u) * 2
    mate = (me_z, me_s, 1 - me_t)

    loads = [
        pltpu.make_async_copy(src, dst, lsem.at[n])
        for n, (src, dst) in enumerate(((sav, savv), (tw, twv), (lat, latv), (sw, swv)))
    ]
    for copy in (loads[1], loads[0]):
        copy.start()
    my_cols = pl.ds(pl.multiple_of(me_t * Cl, Cl), Cl)
    mine = [
        pltpu.make_async_copy(og.at[pl.ds(f * Pl, Pl)], opad.at[pl.ds((f + 1) * Pl, Pl), my_cols], osem.at[f])
        for f in range(F)
    ]
    for copy in mine:
        copy.start()
    for copy in (loads[2], loads[3]):
        copy.start()

    with scope("barrier"):
        barrier = pltpu.get_barrier_semaphore()
        peers = [
            mate, (me_z, sib, me_t), (me_z, sib, 1 - me_t), (me_z, far + me_c, me_t), (me_z, far + 1 - me_c, me_t),
        ]
        count = len(peers) + Z - 1
        for peer in peers:
            pl.semaphore_signal(barrier, inc=1, device_id=peer, device_id_type=MESH)
        for dz in range(1, Z):
            pl.semaphore_signal(
                barrier, inc=1, device_id=(lax.rem(me_z + dz, Z), me_s, me_t), device_id_type=MESH
            )
        pl.semaphore_wait(barrier, count)

    def frame(k):
        return jnp.where(me_u == 0, F - 1 - k, k)

    def block(n, base=0):
        return pl.ds(pl.multiple_of(base + n * Pl, 16), Pl)

    ocopies = []
    for k in range(F):
        f = frame(k)
        copy = pltpu.make_async_remote_copy(
            src_ref=og.at[block(f)], dst_ref=opad.at[block(f, Pl), my_cols],
            send_sem=osend.at[k], recv_sem=orecv.at[k], device_id=mate, device_id_type=MESH,
        )
        copy.start()
        ocopies.append(copy)

    opad[pl.ds(0, Pl), :] = jnp.zeros((Pl, C), BF16)
    opad[pl.ds((F + 1) * Pl, Pl), :] = jnp.zeros((Pl, C), BF16)
    hwide[pl.ds(0, 8), :] = jnp.zeros((8, C), F32)
    hwide[pl.ds(8 + HW, 8), :] = jnp.zeros((8, C), F32)
    for b in range(3):
        hs[b, pl.ds(0, WS), :] = jnp.zeros((WS, C), BF16)
        hs[b, pl.ds(WS + HW, WS), :] = jnp.zeros((WS, C), BF16)
    with scope("load"):
        for copy in loads:
            copy.wait()
        for copy in mine:
            copy.wait()
    savt[...] = savv[...].T
    latt[...] = latv[...].T

    def hidden(f):
        total = None
        for k in range(KT):
            moved = opad[block(f + KT - 1 - k), :]
            term = nt(moved, twv[k])
            total = term if total is None else total + term
        value = total.astype(BF16)
        hsend[block(f), :] = value
        return value

    def landing(n):
        return hs.at[1, block(n, WS), my_cols]

    xcopies = []
    arrived = 0
    for k in range(F - U):
        f = frame(k)
        with scope(f"owait{k}"):
            while arrived < k + 2:
                ocopies[arrived].wait()
                arrived += 1
        with scope(f"hidden{k}"):
            hidden(f)
        slot = lax.rem(f + me_c, 2)
        copy = pltpu.make_async_remote_copy(
            src_ref=hsend.at[block(f)], dst_ref=landing(me_s),
            send_sem=xsend.at[k], recv_sem=xrecv.at[slot],
            device_id=(me_z, f, me_t), device_id_type=MESH,
        )
        copy.start()
        xcopies.append(copy)
    with scope("owait"):
        while arrived < F:
            ocopies[arrived].wait()
            arrived += 1
    with scope("hiddensib"):
        hidden(sib)
    bcopies = [
        pltpu.make_async_remote_copy(
            src_ref=hsend.at[block(sib)], dst_ref=landing(me_s),
            send_sem=bsend.at[n], recv_sem=brecv.at[n],
            device_id=(me_z, sib, t), device_id_type=MESH,
        )
        for n, t in enumerate((1 - me_t, me_t))
    ]
    for copy in bcopies:
        copy.start()
    with scope("hiddenme"):
        value = hidden(me_s)
    ycopies = [
        pltpu.make_async_remote_copy(
            src_ref=hsend.at[block(me_s)], dst_ref=landing(me_s),
            send_sem=ysend.at[0], recv_sem=yrecv.at[0], device_id=mate, device_id_type=MESH,
        )
    ]
    ycopies[0].start()
    hs[1, block(me_s, WS), my_cols] = value

    with scope("relay"):
        for slot in range(2):
            src = far + (me_c if slot == 0 else 1 - me_c)
            pltpu.make_async_remote_copy(
                src_ref=hsend.at[block(me_s)], dst_ref=landing(src),
                send_sem=xsend.at[slot], recv_sem=xrecv.at[slot],
                device_id=(me_z, src, me_t), device_id_type=MESH,
            ).wait_recv()
            copy = pltpu.make_async_remote_copy(
                src_ref=landing(src), dst_ref=landing(src),
                send_sem=ysend.at[1 + slot], recv_sem=yrecv.at[1 + slot], device_id=mate, device_id_type=MESH,
            )
            copy.start()
            ycopies.append(copy)

    sent = {}

    def view(n):
        tap, at, rows = chunks[n]
        return tap, pl.ds(at, rows)

    def start1(n):
        tap, rows = view(n)
        copy = pltpu.make_async_remote_copy(
            src_ref=gsend.at[1 - me_c, :, tap, rows], dst_ref=g1.at[:, tap, rows],
            send_sem=s1s.at[n], recv_sem=s1r.at[n],
            device_id=(me_z, sib, me_t), device_id_type=MESH,
        )
        copy.start()
        sent[1, n] = copy

    def step1(n):
        tap, rows = view(n)
        sent[1, n].wait()
        other = 1 - me_u
        g2s[tap, rows] = (gsend[me_c, other, tap, rows].astype(F32) + g1[other, tap, rows].astype(F32)).astype(BF16)
        copy = pltpu.make_async_remote_copy(
            src_ref=g2s.at[tap, rows], dst_ref=g2r.at[tap, rows],
            send_sem=s2s.at[n], recv_sem=s2r.at[n],
            device_id=(me_z, far + me_c, me_t), device_id_type=MESH,
        )
        copy.start()
        sent[2, n] = copy

    half = Z // 2
    low = me_z < half
    is_end = jnp.logical_or(me_z == 0, me_z == Z - 1)
    is_inner = jnp.logical_or(me_z == half - 1, me_z == half)
    z_in = jnp.where(low, me_z + 1, me_z - 1)
    z_out = jnp.clip(jnp.where(low, me_z - 1, me_z + 1), 0, Z - 1)
    Z_INNER, Z_OUTER = 0, 1

    def hop(n, src, slot, target):
        tap, rows = view(n)
        return pltpu.make_async_remote_copy(
            src_ref=src.at[tap, rows], dst_ref=gzr.at[slot, tap, rows],
            send_sem=s3s.at[slot, n], recv_sem=s3r.at[slot, n],
            device_id=(target, me_s, me_t), device_id_type=MESH,
        )

    def to_inner(n):
        return hop(n, gz, Z_OUTER, z_in)

    def across(n):
        return hop(n, gz, Z_INNER, z_in)

    def to_outer(n):
        return hop(n, gf, Z_INNER, z_out)

    def step2(n):
        tap, rows = view(n)
        sent[2, n].wait()
        total = gsend[me_c, me_u, tap, rows].astype(F32) + g1[me_u, tap, rows].astype(F32)
        total = total + g2r[tap, rows].astype(F32)
        gzf[tap, rows] = total

        @pl.when(is_end)
        def _():
            gz[tap, rows] = total.astype(BF16)
            to_inner(n).start()

    def step3(n):
        tap, rows = view(n)

        @pl.when(is_inner)
        def _():
            to_inner(n).wait_recv()
            gz[tap, rows] = (gzf[tap, rows] + gzr[Z_OUTER, tap, rows].astype(F32)).astype(BF16)
            across(n).start()

    def step4(n):
        tap, rows = view(n)

        @pl.when(is_inner)
        def _():
            across(n).wait_recv()
            gf[tap, rows] = (gz[tap, rows].astype(F32) + gzr[Z_INNER, tap, rows].astype(F32)).astype(BF16)
            to_outer(n).start()

    def step5(n):
        tap, rows = view(n)

        @pl.when(is_end)
        def _():
            across(n).wait_recv()
            gf[tap, rows] = gzr[Z_INNER, tap, rows]

    def finish(n):
        @pl.when(is_inner)
        def _():
            across(n).wait_send()
            to_outer(n).wait_send()

        @pl.when(is_end)
        def _():
            to_inner(n).wait_send()

    def moved_at(tap):
        row, col = tap // 3, tap % 3
        return hs[col, pl.ds((2 - row) * WS, HW), :]

    def gradient(tap):
        if tap < KT:
            part = nn(savt[...], opad[pl.ds((KT - 1 - tap) * Pl, F * Pl), :])
        else:
            part = nn(latt[...], moved_at(tap - KT))
        for s in range(S):
            gsend[s % 2, s // 2, tap] = part[:, s * Cs : (s + 1) * Cs].astype(BF16)
        for n, chunk in enumerate(chunks):
            if chunk[0] == tap:
                start1(n)

    def arrive():
        for copy in ycopies + bcopies:
            copy.wait()
        for copy in xcopies:
            copy.wait_send()

    tile = 4 * WS

    def shift():
        for r in range(0, HW, tile):
            hwide[pl.ds(8 + r, tile), :] = hs[1, pl.ds(WS + r, tile), :].astype(F32)
        column = lax.rem(lax.broadcasted_iota(jnp.int32, (tile, C), 0), WS)
        for b in (-1, 1):
            keep = column != (0 if b == 1 else WS - 1)
            for r in range(0, HW, tile):
                value = hwide[pl.ds(8 + r - b, tile), :]
                hs[b + 1, pl.ds(WS + r, tile), :] = jnp.where(keep, value, 0.0).astype(BF16)

    images = [3 * row + col for col in (1, 0, 2) for row in range(3)]

    def image(n):
        term = nt(moved_at(images[n]), swv[images[n]])
        if n == 0:
            acc[...] = term
        elif n < len(images) - 1:
            acc[...] += term
        else:
            ig[...] = (acc[...] + term).astype(BF16)

    steps = {1: step1, 2: step2, 3: step3, 4: step4, 5: step5, "g": gradient, "i": image}
    for kind, n in order(chunks, KT, len(images), Cl):
        with scope(f"{kind}_{n}"):
            if kind == "h":
                arrive()
            elif kind == "s":
                shift()
            else:
                steps[kind](n)
    with scope("fin"):
        for n in range(len(chunks)):
            finish(n)


def fused(sizes, latents, saved_input, out_grad, temporal_weight, spatial_weight):
    S, T, Z = sizes
    F, Pl, Cl = out_grad.shape[1:]
    KT, _, C = temporal_weight.shape
    taps = KT + spatial_weight.shape[0]
    HW = latents.shape[2]
    Cs = C // S
    U = S // 2
    scale = 1.0 / math.sqrt(Z * F * HS * WS)
    spatial = [KT + 3 * row + col for col in (1, 0, 2) for row in range(3)]
    chunks = pieces_of(list(range(KT)) + spatial, [1] * KT + PARTS, Cl)
    N = len(chunks)
    dims = (S, T, Z, F, Pl, Cl, Cs, chunks, KT)
    V = pltpu.VMEM
    D = pltpu.SemaphoreType.DMA
    hbm = pl.BlockSpec(memory_space=pltpu.HBM)
    vmem = pl.BlockSpec(memory_space=pltpu.VMEM)
    ig, sums = pl.pallas_call(
        functools.partial(kernel, dims),
        out_shape=(
            jax.ShapeDtypeStruct((HW, Cl), BF16),
            jax.ShapeDtypeStruct((taps, Cl, Cs), BF16),
        ),
        in_specs=[hbm] * 5,
        out_specs=(vmem,) * 2,
        scratch_shapes=[
            V((HW, Cl), BF16), V((F * Pl, Cl), BF16), V((KT, Cl, C), BF16), V((taps - KT, Cl, C), BF16),
            V(((F + 2) * Pl, C), BF16), V((F * Pl, Cl), BF16),
            V((HW + 16, C), F32), V((3, HW + 2 * WS, C), BF16),
            V((Cl, F * Pl), BF16), V((Cl, HW), BF16), V((HW, Cl), F32),
            V((2, U, taps, Cl, Cs), BF16), V((U, taps, Cl, Cs), BF16), V((taps, Cl, Cs), BF16),
            V((taps, Cl, Cs), BF16), V((taps, Cl, Cs), BF16), V((taps, Cl, Cs), F32), V((2, taps, Cl, Cs), BF16),
            D((4,)), D((F,)), D((F,)), D((F,)), D((2,)), D((2,)), D((2,)), D((2,)), D((3,)), D((3,)),
            D((N,)), D((N,)), D((N,)), D((N,)),
            D((2, N)), D((2, N)),
        ],
        compiler_params=pltpu.CompilerParams(
            collective_id=0, has_side_effects=True, vmem_limit_bytes=34 * 2**20
        ),
    )(*(
        pltpu.with_memory_space_constraint(value, pltpu.HBM)
        for value in (
            latents.reshape(HW, Cl), saved_input.reshape(F * Pl, Cl), out_grad.reshape(F * Pl, Cl),
            temporal_weight, spatial_weight,
        )
    ))

    def finish(ig_ref, sums_ref, ig_out, tg_out, sg_out):
        ig_out[...] = ig_ref[...]
        tg_out[...] = sums_ref[:KT].astype(F32) * scale
        sg_out[...] = sums_ref[KT:].astype(F32) * scale

    ig, tg, sg = pl.pallas_call(
        finish,
        out_shape=(
            jax.ShapeDtypeStruct((HW, Cl), BF16),
            jax.ShapeDtypeStruct((KT, Cl, Cs), F32),
            jax.ShapeDtypeStruct((taps - KT, Cl, Cs), F32),
        ),
        in_specs=[vmem] * 2,
        out_specs=(vmem,) * 3,
        compiler_params=pltpu.CompilerParams(vmem_limit_bytes=16 * 2**20),
    )(ig, sums)
    return ig.reshape(latents.shape), tg, sg


def plain(latents, saved_input, out_grad, temporal_weight, spatial_weight):
    clips_all = latents.shape[0] * lax.axis_size("clip")
    frames_all = latents.shape[1] * lax.axis_size("sp")
    scale_factor = 1.0 / math.sqrt(clips_all * frames_all * HS * WS)
    frames_count = out_grad.shape[1]
    local_in = temporal_weight.shape[1]
    saved_padded = pad_frames(saved_input)
    block_in = lax.all_gather(out_grad, "tp", axis=3, tiled=True)
    padded = pad_frames(block_in)
    hidden_acc = jnp.zeros(out_grad.shape[:3] + (local_in,), F32)
    parts = []
    for tap_index in range(3):
        shifted = padded[:, 2 - tap_index : 2 - tap_index + frames_count]
        hidden_acc = hidden_acc + jnp.einsum(
            "bfpo,io->bfpi", shifted, temporal_weight[tap_index], preferred_element_type=F32
        )
        window = saved_padded[:, tap_index : tap_index + frames_count]
        parts.append(jnp.einsum("bfpi,bfpo->io", window, block_in, preferred_element_type=F32))
    temporal_local = jnp.stack(parts)
    hidden_grad = hidden_acc.astype(BF16)
    regrouped = lax.all_to_all(hidden_grad, "sp", split_axis=1, concat_axis=2, tiled=True)
    batch = latents.shape[0] * latents.shape[1]
    image_pad = jnp.pad(latents.reshape(batch, HS, WS, local_in), ((0, 0), (1, 1), (1, 1), (0, 0)))
    block_in = lax.all_gather(regrouped, "tp", axis=3, tiled=True)
    whole = block_in.reshape(batch, HS, WS, block_in.shape[3])
    grid = jnp.pad(whole, ((0, 0), (1, 1), (1, 1), (0, 0)))
    input_acc = jnp.zeros((batch, HS, WS, local_in), F32)
    parts = []
    for row in (-1, 0, 1):
        for col in (-1, 0, 1):
            tap_index = 3 * (row + 1) + (col + 1)
            moved = grid[:, 1 - row : 1 - row + HS, 1 - col : 1 - col + WS]
            input_acc = input_acc + jnp.einsum(
                "gabo,co->gabc", moved, spatial_weight[tap_index], preferred_element_type=F32
            )
            window = image_pad[:, 1 + row : 1 + row + HS, 1 + col : 1 + col + WS]
            parts.append(jnp.einsum("gabc,gabo->co", window, whole, preferred_element_type=F32))
    spatial_local = jnp.stack(parts)
    input_grad = input_acc.reshape(latents.shape).astype(BF16)
    temporal_grad, spatial_grad = lax.psum(
        tuple(
            lax.psum_scatter(value * scale_factor, "sp", scatter_dimension=2, tiled=True)
            for value in (temporal_local, spatial_local)
        ),
        "clip",
    )
    return input_grad, temporal_grad, spatial_grad


PARTS = [2, 1, 1, 1, 1, 1, 2, 2, 2]


def solution(mesh):
    sizes = (mesh.shape["sp"], mesh.shape["tp"], mesh.shape["clip"])

    def local(latents, saved_input, out_grad, temporal_weight, spatial_weight):
        S, T, Z = sizes
        cols = temporal_weight.shape[2] // S
        fits = (
            latents.shape[:2] == (1, 1) and S == out_grad.shape[1] == 4 and T == 2 and Z == 4
            and cols % 128 == 0 and out_grad.shape[3] % 128 == 0 and out_grad.shape[2] % WS == 0
        )
        args = (latents, saved_input, out_grad, temporal_weight, spatial_weight)
        return fused(sizes, *args) if fits else plain(*args)

    return jax.shard_map(
        local,
        mesh=mesh,
        in_specs=(
            P("clip", "sp", None, "tp"),
            P("clip", None, "sp", "tp"),
            P("clip", None, "sp", "tp"),
            P(None, "tp", None),
            P(None, "tp", None),
        ),
        out_specs=(P("clip", "sp", None, "tp"), P(None, "tp", "sp"), P(None, "tp", "sp")),
        check_vma=False,
    )
```

time: 68.7 us -> 61.9 us (0.901)
  Pallas kernels: 65.7 us -> 61.1 us
  local copies, waits for them, and re-layouts: 2.17 us -> 0 us
    pallas_call x1, Pallas kernels: 64.3 us -> 59.7 us  [fused(): pl.pallas_call(functools.partial(kernel, dims), out_shape=(jax.ShapeDtype...]
    unnamed x4 -> x0, local copies, waits for them, and re-layouts: 2.17 us -> none
where the time goes in v1:
time: 61.9 us; the launch traced here: 61.7 us
  Pallas kernels  61.1 us (99%)
  between operations  0.64 us (1%)
    pallas_call x1, Pallas kernels, fused(): pl.pallas_call(functools.partial(kernel, dims), out_shape=(jax.ShapeDtype...  59.7 us
    pallas_call x1, Pallas kernels, fused(): pl.pallas_call(finish, out_shape=(jax.ShapeDtypeStruct((HW, Cl), BF16), j...  1.4 us

profile of v1, /device:TPU:0, one launch (start us, length us, event | category | flops | bytes accessed | tf_op | source)
XLA Modules:
  0.0 61.7 jit_solution(3212056506307919909)
XLA Ops:
  0.6 59.7 %shard_map.76 = (bf16[1024,256]{1,0:T(8,128)(2,1)S(1)}, bf16[12,256,128]{2,1,0:T(8,128)(2,1)S(1)}) custom-call(bf16[1024,256]{1,0:T(8,128)(2,1)} %bitcast.4, bf16[1024,256]{1,0:T(8,128)(2,1)} %bitcast.5, bf16[1024,256]{1,0:T(8,128)(2,1)} %bitcast.6, bf16[3,256,512]{2,1,0:T(8,128)(2,1)} %tw.1, bf16[9,256,512]{2,1,0:T(8,128)(2,1)} %sw.1), custom_call_target="tpu_custom_call" | custom-call | tf_op jit(solution)/shard_map/pallas_call | solution.py:418
  60.3 1.4 %shard_map.77 = (bf16[1024,256]{1,0:T(8,128)(2,1)}, f32[3,256,128]{2,1,0:T(8,128)}, f32[9,256,128]{2,1,0:T(8,128)}) custom-call(bf16[1024,256]{1,0:T(8,128)(2,1)S(1)} %get-tuple-element.8.ig_ref, bf16[12,256,128]{2,1,0:T(8,128)(2,1)S(1)} %get-tuple-element.9.sums_ref), custom_call_target="tpu_custom_call" | custom-call | tf_op jit(solution)/shard_map/pallas_call | solution.py:453

commit v2 on v1

v2 whole, which is shorter than its diff:
```python
import contextlib
import functools
import math

import jax
import jax.numpy as jnp
from jax import lax
from jax.experimental import pallas as pl
from jax.experimental.pallas import tpu as pltpu
from jax.sharding import PartitionSpec as P

HS = 32
WS = 32
MESH = pl.DeviceIdType.MESH
F32 = jnp.float32
BF16 = jnp.bfloat16


def pad_frames(values):
    return jnp.pad(values, ((0, 0), (1, 1), (0, 0), (0, 0)))


def nt(a, b):
    return lax.dot_general(a, b, (((1,), (1,)), ((), ())), preferred_element_type=F32)


def nn(a, b):
    return lax.dot_general(a, b, (((1,), (0,)), ((), ())), preferred_element_type=F32)


scope = contextlib.nullcontext


def pieces_of(taps, parts, rows):
    return [(tap, part * (rows // n), rows // n) for tap, n in zip(taps, parts) for part in range(n)]


def order(chunks, first, images, rows):
    hop, core_hop, link, core = 1.8, 0.65, 1.39, 0.44
    arrival = 3.0
    now, free = -2.0, {"core": 0.0, "x": -2.0, "z": 0.0, "across": 0.0, "back": 0.0}
    pending, out = {}, []

    def send(name, n, step):
        part = chunks[n][2] / rows
        free[name] = max(free[name], now) + (core if name == "core" else link) * part
        pending[step, n] = free[name] + (core_hop if name == "core" else hop)

    taps = list(dict.fromkeys(tap for tap, _, _ in chunks))
    late, filler = taps[first:], ["h", "s"] + list(range(images))
    for n, chunk in enumerate(chunks):
        if chunk[0] in taps[:first]:
            send("x", n, 2)
    now = 0.0
    while pending or late or filler:
        ready = sorted((at, key) for key, at in pending.items() if at <= now)
        if ready:
            at, (step, n) = ready[0]
            now += 0.06 * chunks[n][2] / rows
            del pending[step, n]
            out.append((step, n))
            if step < 5:
                send(("core", "x", "z", "across", "back")[step], n, step + 1)
            continue
        soon = min(pending.values()) if pending else 1e9
        if late:
            tap = late.pop(0)
            out.append(("g", tap))
            now += 0.45
            for n, chunk in enumerate(chunks):
                if chunk[0] == tap:
                    send("core", n, 1)
        elif filler and now >= arrival and (soon > now + 0.25 or not pending):
            kind = filler.pop(0)
            out.append((kind, 0) if isinstance(kind, str) else ("i", kind))
            now += 0.1 if kind == "h" else 0.58
        else:
            now = max(now, soon if not filler or now >= arrival else min(soon, arrival))
    return out


def kernel(
    dims, lat, sav, og, tw, sw, ig, gf,
    savv, twv, twx, swv, opad, hid, savt, latl, lwide, latt, hwide, hs, acc,
    gsend, g1, g2s, g2r, gz, gzf, gzr,
    lsem, osend, orecv, osem, xsend, xrecv, bsem, ysend, yrecv,
    lxsend, lxrecv, wysem, wzsend, wzrecv, wcsend, wcrecv,
    s1s, s1r, s2s, s2r, s3s, s3r,
):
    S, T, Z, F, Pl, Cl, Cs, chunks, KT = dims
    U = S // 2
    HW = S * Pl
    C = T * Cl
    R = Pl // WS
    me_s, me_t, me_z = lax.axis_index("sp"), lax.axis_index("tp"), lax.axis_index("clip")
    me_u, me_c = me_s // 2, lax.rem(me_s, 2)
    sib = me_u * 2 + 1 - me_c
    far = (1 - me_u) * 2
    mate = (me_z, me_s, 1 - me_t)
    near = (me_z, sib, me_t)
    others = (sib, far + me_c, far + 1 - me_c)

    def remote(src, dst, send, recv, device):
        return pltpu.make_async_remote_copy(
            src_ref=src, dst_ref=dst, send_sem=send, recv_sem=recv, device_id=device, device_id_type=MESH
        )

    def block(n, base=0):
        return pl.ds(pl.multiple_of(base + n * Pl, 16), Pl)

    def window(n):
        at = jnp.clip(n * R - 1, 0, HW // WS - R - 2)
        return (
            pl.ds(pl.multiple_of(at * WS, WS), (R + 2) * WS),
            pl.ds(pl.multiple_of((at - n * R + 2) * WS, WS), (R + 2) * WS),
        )

    my_cols = pl.ds(pl.multiple_of(me_t * Cl, Cl), Cl)
    mate_cols = pl.ds(pl.multiple_of((1 - me_t) * Cl, Cl), Cl)
    loads = [
        pltpu.make_async_copy(src, dst, lsem.at[n]) for n, (src, dst) in enumerate(((tw, twv), (sav, savv), (sw, swv)))
    ]
    mine = [
        pltpu.make_async_copy(og.at[pl.ds(f * Pl, Pl)], opad.at[pl.ds((f + 1) * Pl, Pl), my_cols], osem.at[f])
        for f in range(F)
    ]
    for f in range(F):
        latl[f, pl.ds(WS, WS), :] = jnp.zeros((WS, Cl), BF16)
        latl[f, pl.ds((R + 2) * WS, WS), :] = jnp.zeros((WS, Cl), BF16)
    for copy in mine + loads:
        copy.start()

    with scope("barrier"):
        barrier = pltpu.get_barrier_semaphore()
        peers = [mate, near, (me_z, others[1], me_t), (me_z, others[2], me_t)]
        count = len(peers) + Z - 1
        for peer in peers:
            pl.semaphore_signal(barrier, inc=1, device_id=peer, device_id_type=MESH)
        for dz in range(1, Z):
            pl.semaphore_signal(
                barrier, inc=1, device_id=(lax.rem(me_z + dz, Z), me_s, me_t), device_id_type=MESH
            )
        pl.semaphore_wait(barrier, count)

    def frame(k):
        return jnp.where(me_u == 0, F - 1 - k, k)

    share = Cl // (2 * Z)

    def slice_of(z, c):
        return pl.ds(pl.multiple_of((z * 2 + c) * share, 16), share)

    here = slice_of(me_z, me_c)
    wy = remote(tw.at[:, here], twx.at[:, here], wysem.at[0], wysem.at[1], mate)
    wy.start()
    ocopies = []
    for k in range(F):
        f = frame(k)
        copy = remote(og.at[block(f)], opad.at[block(f, Pl), my_cols], osend.at[k], orecv.at[k], mate)
        copy.start()
        ocopies.append(copy)
    lcopies = []
    for n in (1, 2, 0):
        src, dst = window(others[n])
        copy = remote(lat.at[src], latl.at[me_s, dst], lxsend.at[n], lxrecv.at[n], (me_z, others[n], me_t))
        copy.start()
        lcopies.append(copy)
    src, dst = window(me_s)
    own = pltpu.make_async_copy(lat.at[src], latl.at[me_s, dst], lsem.at[3])
    own.start()

    opad[pl.ds(0, Pl), :] = jnp.zeros((Pl, C), BF16)
    opad[pl.ds((F + 1) * Pl, Pl), :] = jnp.zeros((Pl, C), BF16)
    hwide[pl.ds(0, 8), :] = jnp.zeros((8, C), F32)
    hwide[pl.ds(8 + HW, 8), :] = jnp.zeros((8, C), F32)
    for b in range(3):
        hs[b, pl.ds(0, WS), :] = jnp.zeros((WS, C), BF16)
        hs[b, pl.ds(WS + HW, WS), :] = jnp.zeros((WS, C), BF16)
    with scope("load"):
        for copy in mine + loads:
            copy.wait()
    savt[...] = savv[...].T

    with scope("wy"):
        wy.wait()
    part = twx.at[:, here]
    wcopies = [remote(part, part, wcsend.at[0], wcrecv.at[0], near)]
    wcopies[0].start()
    wzcopies = []
    for dz in range(1, Z):
        copy = remote(
            part, part, wzsend.at[dz - 1], wzrecv.at[dz - 1], (lax.rem(me_z + dz, Z), me_s, me_t)
        )
        copy.start()
        wzcopies.append(copy)

    def pass_on(dz):
        wzcopies[dz - 1].wait_recv()
        piece = twx.at[:, slice_of(lax.rem(me_z + Z - dz, Z), me_c)]
        copy = remote(piece, piece, wcsend.at[dz], wcrecv.at[dz], near)
        copy.start()
        wcopies.append(copy)

    with scope("lwait"):
        own.wait()
        for copy in lcopies:
            copy.wait()
    span = (R + 2) * WS
    column = lax.rem(lax.broadcasted_iota(jnp.int32, (span, Cl), 0), WS)

    def latents_of(f):
        lwide[...] = latl[f].astype(F32)
        for b in range(3):
            if b == 1:
                value = latl[f, pl.ds(WS, span), :]
            else:
                value = lwide[pl.ds(WS + b - 1, span), :]
                value = jnp.where(column != (WS - 1 if b == 2 else 0), value, 0.0).astype(BF16)
            for row in range(3):
                latt[3 * row + b, :, pl.ds(f * Pl, Pl)] = value[row * WS : row * WS + Pl].T

    def landing(n):
        return hs.at[1, block(n, WS), my_cols]

    def hidden(weights, at, size):
        total = None
        for k in range(KT):
            term = nt(opad[pl.ds(pl.multiple_of(at + (KT - 1 - k) * Pl, 16), size), :], weights[k])
            total = term if total is None else total + term
        return total.astype(BF16)

    xcopies = []
    arrived = 0

    def take(n):
        nonlocal arrived
        with scope(f"owait{n}"):
            while arrived < n:
                ocopies[arrived].wait()
                arrived += 1

    for k in range(F - U):
        f = frame(k)
        with scope(f"lshift{k}"):
            for part_f in range(k * U, (k + 1) * U):
                latents_of(part_f)
        take(k + 2)
        with scope(f"hidden{k}"):
            hid[block(f), my_cols] = hidden(twv, f * Pl, Pl)
        copy = remote(
            hid.at[block(f), my_cols], landing(me_s), xsend.at[k], xrecv.at[lax.rem(f + me_c, 2)], (me_z, f, me_t)
        )
        copy.start()
        xcopies.append(copy)
        with scope(f"pass{k}"):
            pass_on(1 if k == 0 else Z - 1)
    take(F)

    sent = {}

    def view(n):
        tap, at, rows = chunks[n]
        return tap, pl.ds(at, rows)

    def start1(n):
        at = view(n)
        sent[1, n] = remote(gsend.at[(1 - me_c, slice(None)) + at], g1.at[(slice(None),) + at], s1s.at[n], s1r.at[n], near)
        sent[1, n].start()

    def step1(n):
        at = view(n)
        sent[1, n].wait()
        other = 1 - me_u
        g2s[at] = (gsend[(me_c, other) + at].astype(F32) + g1[(other,) + at].astype(F32)).astype(BF16)
        sent[2, n] = remote(g2s.at[at], g2r.at[at], s2s.at[n], s2r.at[n], (me_z, others[1], me_t))
        sent[2, n].start()

    half = Z // 2
    low = me_z < half
    is_end = jnp.logical_or(me_z == 0, me_z == Z - 1)
    is_inner = jnp.logical_or(me_z == half - 1, me_z == half)
    z_in = jnp.where(low, me_z + 1, me_z - 1)
    z_out = jnp.clip(jnp.where(low, me_z - 1, me_z + 1), 0, Z - 1)
    Z_INNER, Z_OUTER = 0, 1

    def hop(n, src, slot, target):
        at = view(n)
        return remote(src.at[at], gzr.at[(slot,) + at], s3s.at[slot, n], s3r.at[slot, n], (target, me_s, me_t))

    def to_inner(n):
        return hop(n, gz, Z_OUTER, z_in)

    def across(n):
        return hop(n, gz, Z_INNER, z_in)

    def to_outer(n):
        return hop(n, gf, Z_INNER, z_out)

    def step2(n):
        at = view(n)
        sent[2, n].wait()
        total = gsend[(me_c, me_u) + at].astype(F32) + g1[(me_u,) + at].astype(F32)
        total = total + g2r[at].astype(F32)
        gzf[at] = total

        @pl.when(is_end)
        def _():
            gz[at] = total.astype(BF16)
            to_inner(n).start()

    def step3(n):
        at = view(n)

        @pl.when(is_inner)
        def _():
            to_inner(n).wait_recv()
            gz[at] = (gzf[at] + gzr[(Z_OUTER,) + at].astype(F32)).astype(BF16)
            across(n).start()

    def step4(n):
        at = view(n)

        @pl.when(is_inner)
        def _():
            across(n).wait_recv()
            value = (gz[at].astype(F32) + gzr[(Z_INNER,) + at].astype(F32)).astype(BF16)
            gf[at] = value
            to_outer(n).start()

    def step5(n):
        at = view(n)

        @pl.when(is_end)
        def _():
            across(n).wait_recv()
            gf[at] = gzr[(Z_INNER,) + at]

    def finish(n):
        @pl.when(is_inner)
        def _():
            across(n).wait_send()
            to_outer(n).wait_send()

        @pl.when(is_end)
        def _():
            to_inner(n).wait_send()

    def gradient(tap):
        if tap < KT:
            part = nn(savt[...], opad[pl.ds((KT - 1 - tap) * Pl, F * Pl), :])
        else:
            part = nn(latt[tap - KT], hid[...])
        for s in range(S):
            gsend[s % 2, s // 2, tap] = part[:, s * Cs : (s + 1) * Cs].astype(BF16)
        for n, chunk in enumerate(chunks):
            if chunk[0] == tap:
                start1(n)

    early = [n for n, chunk in enumerate(chunks) if chunk[0] < KT]
    for tap in range(KT):
        with scope(f"g_{tap}"):
            gradient(tap)
    with scope("passlast"):
        for dz in range(2, Z - 1):
            pass_on(dz)
    with scope("early0"):
        step1(early[0])
    with scope("hiddenown"):
        for k in range(F - U, F):
            f = frame(k)
            hid[block(f), my_cols] = hidden(twv, f * Pl, Pl)
    with scope("early"):
        for n in early[1:]:
            step1(n)
    with scope("wwait"):
        for copy in wcopies:
            copy.wait()
        for copy in wzcopies:
            copy.wait_send()
    with scope("hiddenrest"):
        hid[:, mate_cols] = hidden(twx, 0, F * Pl)
    to_sib = remote(hid.at[block(sib)], hs.at[1, block(me_s, WS)], bsem.at[0], bsem.at[1], near)
    to_sib.start()
    ycopies = []
    with scope("relay"):
        for slot in range(2):
            source = others[1 + slot]
            remote(
                landing(source), landing(source), xsend.at[slot], xrecv.at[slot], (me_z, source, me_t)
            ).wait_recv()
            copy = remote(landing(source), landing(source), ysend.at[slot], yrecv.at[slot], mate)
            copy.start()
            ycopies.append(copy)

    def arrive():
        to_sib.wait()
        for copy in ycopies:
            copy.wait()
        for copy in xcopies:
            copy.wait_send()
        hs[1, block(me_s, WS), :] = hid[block(me_s), :]

    tile = 4 * WS

    def shift():
        for r in range(0, HW, tile):
            hwide[pl.ds(8 + r, tile), :] = hs[1, pl.ds(WS + r, tile), :].astype(F32)
        column = lax.rem(lax.broadcasted_iota(jnp.int32, (tile, C), 0), WS)
        for b in (-1, 1):
            keep = column != (0 if b == 1 else WS - 1)
            for r in range(0, HW, tile):
                value = hwide[pl.ds(8 + r - b, tile), :]
                hs[b + 1, pl.ds(WS + r, tile), :] = jnp.where(keep, value, 0.0).astype(BF16)

    images = swv.shape[0]

    def image(tap):
        row, col = tap // 3, tap % 3
        term = nt(hs[col, pl.ds((2 - row) * WS, HW), :], swv[tap])
        if tap == 0:
            acc[...] = term
        elif tap < images - 1:
            acc[...] += term
        else:
            ig[...] = (acc[...] + term).astype(BF16)

    steps = {1: step1, 2: step2, 3: step3, 4: step4, 5: step5, "g": gradient, "i": image}
    for kind, n in order(chunks, KT, images, Cl):
        with scope(f"{kind}_{n}"):
            if kind == "h":
                arrive()
            elif kind == "s":
                shift()
            else:
                steps[kind](n)
    with scope("fin"):
        for n in range(len(chunks)):
            finish(n)


def fused(sizes, latents, saved_input, out_grad, temporal_weight, spatial_weight):
    S, T, Z = sizes
    F, Pl, Cl = out_grad.shape[1:]
    KT, _, C = temporal_weight.shape
    taps = KT + spatial_weight.shape[0]
    HW = latents.shape[2]
    Cs = C // S
    U = S // 2
    scale = 1.0 / math.sqrt(Z * F * HS * WS)
    chunks = pieces_of(list(range(taps)), [1] * KT + PARTS, Cl)
    N = len(chunks)
    dims = (S, T, Z, F, Pl, Cl, Cs, chunks, KT)
    V = pltpu.VMEM
    D = pltpu.SemaphoreType.DMA
    hbm = pl.BlockSpec(memory_space=pltpu.HBM)
    vmem = pl.BlockSpec(memory_space=pltpu.VMEM)
    ig, sums = pl.pallas_call(
        functools.partial(kernel, dims),
        out_shape=(
            jax.ShapeDtypeStruct((HW, Cl), BF16),
            jax.ShapeDtypeStruct((taps, Cl, Cs), BF16),
        ),
        in_specs=[hbm] * 5,
        out_specs=(vmem,) * 2,
        scratch_shapes=[
            V((F * Pl, Cl), BF16), V((KT, Cl, C), BF16), V((KT, Cl, C), BF16), V((taps - KT, Cl, C), BF16),
            V(((F + 2) * Pl, C), BF16), V((F * Pl, C), BF16), V((Cl, F * Pl), BF16),
            V((F, Pl + 4 * WS, Cl), BF16), V((Pl + 4 * WS, Cl), F32), V((taps - KT, Cl, F * Pl), BF16),
            V((HW + 16, C), F32), V((3, HW + 2 * WS, C), BF16), V((HW, Cl), F32),
            V((2, U, taps, Cl, Cs), BF16), V((U, taps, Cl, Cs), BF16), V((taps, Cl, Cs), BF16),
            V((taps, Cl, Cs), BF16), V((taps, Cl, Cs), BF16), V((taps, Cl, Cs), F32), V((2, taps, Cl, Cs), BF16),
            D((4,)), D((F,)), D((F,)), D((F,)), D((U,)), D((U,)), D((2,)), D((2,)), D((2,)),
            D((3,)), D((3,)), D((2,)), D((Z - 1,)), D((Z - 1,)), D((Z,)), D((Z,)),
            D((N,)), D((N,)), D((N,)), D((N,)),
            D((2, N)), D((2, N)),
        ],
        compiler_params=pltpu.CompilerParams(
            collective_id=0, has_side_effects=True, vmem_limit_bytes=40 * 2**20
        ),
    )(*(
        pltpu.with_memory_space_constraint(value, pltpu.HBM)
        for value in (
            latents.reshape(HW, Cl), saved_input.reshape(F * Pl, Cl), out_grad.reshape(F * Pl, Cl),
            temporal_weight, spatial_weight,
        )
    ))

    def finish(ig_ref, sums_ref, ig_out, tg_out, sg_out):
        ig_out[...] = ig_ref[...]
        tg_out[...] = sums_ref[:KT].astype(F32) * scale
        sg_out[...] = sums_ref[KT:].astype(F32) * scale

    ig, tg, sg = pl.pallas_call(
        finish,
        out_shape=(
            jax.ShapeDtypeStruct((HW, Cl), BF16),
            jax.ShapeDtypeStruct((KT, Cl, Cs), F32),
            jax.ShapeDtypeStruct((taps - KT, Cl, Cs), F32),
        ),
        in_specs=[vmem] * 2,
        out_specs=(vmem,) * 3,
        compiler_params=pltpu.CompilerParams(vmem_limit_bytes=16 * 2**20),
    )(ig, sums)
    return ig.reshape(latents.shape), tg, sg


def plain(latents, saved_input, out_grad, temporal_weight, spatial_weight):
    clips_all = latents.shape[0] * lax.axis_size("clip")
    frames_all = latents.shape[1] * lax.axis_size("sp")
    scale_factor = 1.0 / math.sqrt(clips_all * frames_all * HS * WS)
    frames_count = out_grad.shape[1]
    local_in = temporal_weight.shape[1]
    saved_padded = pad_frames(saved_input)
    block_in = lax.all_gather(out_grad, "tp", axis=3, tiled=True)
    padded = pad_frames(block_in)
    hidden_acc = jnp.zeros(out_grad.shape[:3] + (local_in,), F32)
    parts = []
    for tap_index in range(3):
        shifted = padded[:, 2 - tap_index : 2 - tap_index + frames_count]
        hidden_acc = hidden_acc + jnp.einsum(
            "bfpo,io->bfpi", shifted, temporal_weight[tap_index], preferred_element_type=F32
        )
        window = saved_padded[:, tap_index : tap_index + frames_count]
        parts.append(jnp.einsum("bfpi,bfpo->io", window, block_in, preferred_element_type=F32))
    temporal_local = jnp.stack(parts)
    hidden_grad = hidden_acc.astype(BF16)
    regrouped = lax.all_to_all(hidden_grad, "sp", split_axis=1, concat_axis=2, tiled=True)
    batch = latents.shape[0] * latents.shape[1]
    image_pad = jnp.pad(latents.reshape(batch, HS, WS, local_in), ((0, 0), (1, 1), (1, 1), (0, 0)))
    block_in = lax.all_gather(regrouped, "tp", axis=3, tiled=True)
    whole = block_in.reshape(batch, HS, WS, block_in.shape[3])
    grid = jnp.pad(whole, ((0, 0), (1, 1), (1, 1), (0, 0)))
    input_acc = jnp.zeros((batch, HS, WS, local_in), F32)
    parts = []
    for row in (-1, 0, 1):
        for col in (-1, 0, 1):
            tap_index = 3 * (row + 1) + (col + 1)
            moved = grid[:, 1 - row : 1 - row + HS, 1 - col : 1 - col + WS]
            input_acc = input_acc + jnp.einsum(
                "gabo,co->gabc", moved, spatial_weight[tap_index], preferred_element_type=F32
            )
            window = image_pad[:, 1 + row : 1 + row + HS, 1 + col : 1 + col + WS]
            parts.append(jnp.einsum("gabc,gabo->co", window, whole, preferred_element_type=F32))
    spatial_local = jnp.stack(parts)
    input_grad = input_acc.reshape(latents.shape).astype(BF16)
    temporal_grad, spatial_grad = lax.psum(
        tuple(
            lax.psum_scatter(value * scale_factor, "sp", scatter_dimension=2, tiled=True)
            for value in (temporal_local, spatial_local)
        ),
        "clip",
    )
    return input_grad, temporal_grad, spatial_grad


PARTS = [2, 1, 1, 1, 1, 1, 1, 2, 2]


def solution(mesh):
    sizes = (mesh.shape["sp"], mesh.shape["tp"], mesh.shape["clip"])

    def local(latents, saved_input, out_grad, temporal_weight, spatial_weight):
        S, T, Z = sizes
        cols = temporal_weight.shape[2] // S
        fits = (
            latents.shape[:2] == (1, 1) and S == out_grad.shape[1] == 4 and T == 2 and Z == 4
            and cols % 128 == 0 and out_grad.shape[3] % 256 == 0 and out_grad.shape[2] % 128 == 0
            and latents.shape[2] == HS * WS == S * out_grad.shape[2]
        )
        args = (latents, saved_input, out_grad, temporal_weight, spatial_weight)
        return fused(sizes, *args) if fits else plain(*args)

    return jax.shard_map(
        local,
        mesh=mesh,
        in_specs=(
            P("clip", "sp", None, "tp"),
            P("clip", None, "sp", "tp"),
            P("clip", None, "sp", "tp"),
            P(None, "tp", None),
            P(None, "tp", None),
        ),
        out_specs=(P("clip", "sp", None, "tp"), P(None, "tp", "sp"), P(None, "tp", "sp")),
        check_vma=False,
    )
```

time: 61.9 us -> 57.1 us (0.922)
  Pallas kernels: 61.1 us -> 56.3 us
    pallas_call x1, Pallas kernels: 59.7 us -> 54.9 us  [fused(): pl.pallas_call(functools.partial(kernel, dims), out_shape=(jax.ShapeDtype...]
where the time goes in v2:
time: 57.1 us; the launch traced here: 56.9 us
  Pallas kernels  56.3 us (99%)
  between operations  0.64 us (1%)
    pallas_call x1, Pallas kernels, fused(): pl.pallas_call(functools.partial(kernel, dims), out_shape=(jax.ShapeDtype...  54.9 us
    pallas_call x1, Pallas kernels, fused(): pl.pallas_call(finish, out_shape=(jax.ShapeDtypeStruct((HW, Cl), BF16), j...  1.4 us

profile of v2, /device:TPU:0, one launch (start us, length us, event | category | flops | bytes accessed | tf_op | source)
XLA Modules:
  0.0 56.9 jit_solution(2501948788720773196)
XLA Ops:
  0.6 54.9 %shard_map.76 = (bf16[1024,256]{1,0:T(8,128)(2,1)S(1)}, bf16[12,256,128]{2,1,0:T(8,128)(2,1)S(1)}) custom-call(bf16[1024,256]{1,0:T(8,128)(2,1)} %bitcast.4, bf16[1024,256]{1,0:T(8,128)(2,1)} %bitcast.5, bf16[1024,256]{1,0:T(8,128)(2,1)} %bitcast.6, bf16[3,256,512]{2,1,0:T(8,128)(2,1)} %tw.1, bf16[9,256,512]{2,1,0:T(8,128)(2,1)} %sw.1), custom_call_target="tpu_custom_call" | custom-call | tf_op jit(solution)/shard_map/pallas_call | solution.py:457
  55.5 1.4 %shard_map.77 = (bf16[1024,256]{1,0:T(8,128)(2,1)}, f32[3,256,128]{2,1,0:T(8,128)}, f32[9,256,128]{2,1,0:T(8,128)}) custom-call(bf16[1024,256]{1,0:T(8,128)(2,1)S(1)} %get-tuple-element.8.ig_ref, bf16[12,256,128]{2,1,0:T(8,128)(2,1)S(1)} %get-tuple-element.9.sums_ref), custom_call_target="tpu_custom_call" | custom-call | tf_op jit(solution)/shard_map/pallas_call | solution.py:493

commit v3 on v2

--- a/solution.py
+++ b/solution.py
@@ -36,9 +36,9 @@
 
 
 def order(chunks, first, images, rows):
-    hop, core_hop, link, core = 1.8, 0.65, 1.39, 0.44
-    arrival = 3.0
-    now, free = -2.0, {"core": 0.0, "x": -2.0, "z": 0.0, "across": 0.0, "back": 0.0}
+    hop, core_hop, link, core = HOP, 0.65, 1.39, 0.44
+    arrival = 8.0
+    now, free = START, {"core": 0.0, "x": START, "z": 0.0, "across": 0.0, "back": 0.0}
     pending, out = {}, []
 
     def send(name, n, step):
@@ -66,28 +66,27 @@
         if late:
             tap = late.pop(0)
             out.append(("g", tap))
-            now += 0.45
+            now += 0.7 if len(taps) - first - len(late) <= 3 else 0.45
             for n, chunk in enumerate(chunks):
                 if chunk[0] == tap:
                     send("core", n, 1)
         elif filler and now >= arrival and (soon > now + 0.25 or not pending):
             kind = filler.pop(0)
             out.append((kind, 0) if isinstance(kind, str) else ("i", kind))
-            now += 0.1 if kind == "h" else 0.58
+            now += 0.1 if kind == "h" else 0.55 if kind == "s" else 0.3
         else:
             now = max(now, soon if not filler or now >= arrival else min(soon, arrival))
     return out
 
 
 def kernel(
-    dims, lat, sav, og, tw, sw, ig, gf,
-    savv, twv, twx, swv, opad, hid, savt, latl, lwide, latt, hwide, hs, acc,
+    dims, lat, sav, og, tw, sw, ig_out, sums_out,
+    savv, twv, twx, swv, opad, hid, savt, latl, lwide, latt, hwide, hs, acc, ig, gf, sums,
     gsend, g1, g2s, g2r, gz, gzf, gzr,
-    lsem, osend, orecv, osem, xsend, xrecv, bsem, ysend, yrecv,
-    lxsend, lxrecv, wysem, wzsend, wzrecv, wcsend, wcrecv,
-    s1s, s1r, s2s, s2r, s3s, s3r,
+    lsem, osend, orecv, osem, xsend, xrecv, bsem, ysem, lxsem, wysem, wzsend, wzrecv, wxsend, wxrecv, wcsem,
+    s1s, s1r, s2s, s2r, s3s, s3r, isem, rsem,
 ):
-    S, T, Z, F, Pl, Cl, Cs, chunks, KT = dims
+    S, T, Z, F, Pl, Cl, Cs, scale, chunks, KT = dims
     U = S // 2
     HW = S * Pl
     C = T * Cl
@@ -121,9 +120,10 @@
         pltpu.make_async_copy(src, dst, lsem.at[n]) for n, (src, dst) in enumerate(((tw, twv), (sav, savv), (sw, swv)))
     ]
     mine = [
-        pltpu.make_async_copy(og.at[pl.ds(f * Pl, Pl)], opad.at[pl.ds((f + 1) * Pl, Pl), my_cols], osem.at[f])
+        pltpu.make_async_copy(og.at[pl.ds(f * Pl, Pl)], opad.at[pl.ds((f + 1) * Pl, Pl), my_cols], osem)
         for f in range(F)
     ]
+    own_og = pltpu.make_async_copy(og, opad.at[pl.ds(Pl, F * Pl), my_cols], osem)
     for f in range(F):
         latl[f, pl.ds(WS, WS), :] = jnp.zeros((WS, Cl), BF16)
         latl[f, pl.ds((R + 2) * WS, WS), :] = jnp.zeros((WS, Cl), BF16)
@@ -145,26 +145,27 @@
     def frame(k):
         return jnp.where(me_u == 0, F - 1 - k, k)
 
-    share = Cl // (2 * Z)
-
-    def slice_of(z, c):
-        return pl.ds(pl.multiple_of((z * 2 + c) * share, 16), share)
-
-    here = slice_of(me_z, me_c)
+    share = Cl // (2 * Z * U)
+
+    def slice_of(u, c, z):
+        return twx.at[:, pl.ds(pl.multiple_of(((u * 2 + c) * Z + z) * share, 16), share)]
+
+    def slices(n):
+        return twx.at[:, pl.ds(0, n * share)]
+
+    here = pl.ds(pl.multiple_of(((me_u * 2 + me_c) * Z + me_z) * share, 16), share)
+    x_mate = (me_z, others[1], me_t)
     wy = remote(tw.at[:, here], twx.at[:, here], wysem.at[0], wysem.at[1], mate)
     wy.start()
     ocopies = []
     for k in range(F):
         f = frame(k)
-        copy = remote(og.at[block(f)], opad.at[block(f, Pl), my_cols], osend.at[k], orecv.at[k], mate)
+        copy = remote(og.at[block(f)], opad.at[block(f, Pl), my_cols], osend, orecv.at[k], mate)
         copy.start()
         ocopies.append(copy)
-    lcopies = []
     for n in (1, 2, 0):
         src, dst = window(others[n])
-        copy = remote(lat.at[src], latl.at[me_s, dst], lxsend.at[n], lxrecv.at[n], (me_z, others[n], me_t))
-        copy.start()
-        lcopies.append(copy)
+        remote(lat.at[src], latl.at[me_s, dst], lxsem.at[0], lxsem.at[1], (me_z, others[n], me_t)).start()
     src, dst = window(me_s)
     own = pltpu.make_async_copy(lat.at[src], latl.at[me_s, dst], lsem.at[3])
     own.start()
@@ -177,34 +178,41 @@
         hs[b, pl.ds(0, WS), :] = jnp.zeros((WS, C), BF16)
         hs[b, pl.ds(WS + HW, WS), :] = jnp.zeros((WS, C), BF16)
     with scope("load"):
-        for copy in mine + loads:
+        own_og.wait()
+        for copy in loads:
             copy.wait()
     savt[...] = savv[...].T
 
+    def pass_x(n):
+        piece = slice_of(me_u, me_c, lax.rem(me_z + Z - n, Z))
+        remote(piece, piece, wxsend, wxrecv.at[n], x_mate).start()
+        remote(piece, piece, wcsem.at[0], wcsem.at[1], near).start()
+
+    def pass_z(n):
+        piece = slice_of(me_u, me_c, lax.rem(me_z + Z - n, Z))
+        remote(piece, piece, wzsend, wzrecv.at[n - 1], (lax.rem(me_z + n, Z), me_s, me_t)).wait_recv()
+        pass_x(n)
+
+    def pass_core(n):
+        piece = slice_of(1 - me_u, me_c, lax.rem(me_z + Z - n, Z))
+        remote(piece, piece, wxsend, wxrecv.at[n], x_mate).wait_recv()
+        remote(piece, piece, wcsem.at[0], wcsem.at[1], near).start()
+
     with scope("wy"):
         wy.wait()
-    part = twx.at[:, here]
-    wcopies = [remote(part, part, wcsend.at[0], wcrecv.at[0], near)]
-    wcopies[0].start()
-    wzcopies = []
-    for dz in range(1, Z):
-        copy = remote(
-            part, part, wzsend.at[dz - 1], wzrecv.at[dz - 1], (lax.rem(me_z + dz, Z), me_s, me_t)
-        )
-        copy.start()
-        wzcopies.append(copy)
-
-    def pass_on(dz):
-        wzcopies[dz - 1].wait_recv()
-        piece = twx.at[:, slice_of(lax.rem(me_z + Z - dz, Z), me_c)]
-        copy = remote(piece, piece, wcsend.at[dz], wcrecv.at[dz], near)
-        copy.start()
-        wcopies.append(copy)
-
+    for dz in (1, Z - 1, 2):
+        piece = slice_of(me_u, me_c, me_z)
+        remote(piece, piece, wzsend, wzrecv.at[dz - 1], (lax.rem(me_z + dz, Z), me_s, me_t)).start()
+    pass_x(0)
+
+    with scope("passz"):
+        pass_z(1)
+        pass_z(Z - 1)
     with scope("lwait"):
         own.wait()
-        for copy in lcopies:
-            copy.wait()
+        part = lat.at[pl.ds(0, len(others) * (R + 2) * WS)]
+        remote(part, part, lxsem.at[0], lxsem.at[1], near).wait()
+
     span = (R + 2) * WS
     column = lax.rem(lax.broadcasted_iota(jnp.int32, (span, Cl), 0), WS)
 
@@ -229,14 +237,13 @@
             total = term if total is None else total + term
         return total.astype(BF16)
 
-    xcopies = []
     arrived = 0
 
     def take(n):
         nonlocal arrived
         with scope(f"owait{n}"):
             while arrived < n:
-                ocopies[arrived].wait()
+                ocopies[arrived].wait_recv()
                 arrived += 1
 
     for k in range(F - U):
@@ -244,16 +251,19 @@
         with scope(f"lshift{k}"):
             for part_f in range(k * U, (k + 1) * U):
                 latents_of(part_f)
+        if k == 0:
+            with scope("passz2"):
+                pass_z(2)
         take(k + 2)
         with scope(f"hidden{k}"):
             hid[block(f), my_cols] = hidden(twv, f * Pl, Pl)
         copy = remote(
-            hid.at[block(f), my_cols], landing(me_s), xsend.at[k], xrecv.at[lax.rem(f + me_c, 2)], (me_z, f, me_t)
+            hid.at[block(f), my_cols], landing(me_s), xsend, xrecv.at[lax.rem(f + me_c, 2)], (me_z, f, me_t)
         )
         copy.start()
-        xcopies.append(copy)
         with scope(f"pass{k}"):
-            pass_on(1 if k == 0 else Z - 1)
+            for n in ((0, 1), (Z - 1, 2))[k]:
+                pass_core(n)
     take(F)
 
     sent = {}
@@ -264,15 +274,15 @@
 
     def start1(n):
         at = view(n)
-        sent[1, n] = remote(gsend.at[(1 - me_c, slice(None)) + at], g1.at[(slice(None),) + at], s1s.at[n], s1r.at[n], near)
+        sent[1, n] = remote(gsend.at[(1 - me_c, slice(None)) + at], g1.at[(slice(None),) + at], s1s, s1r.at[n], near)
         sent[1, n].start()
 
     def step1(n):
         at = view(n)
-        sent[1, n].wait()
+        sent[1, n].wait_recv()
         other = 1 - me_u
         g2s[at] = (gsend[(me_c, other) + at].astype(F32) + g1[(other,) + at].astype(F32)).astype(BF16)
-        sent[2, n] = remote(g2s.at[at], g2r.at[at], s2s.at[n], s2r.at[n], (me_z, others[1], me_t))
+        sent[2, n] = remote(g2s.at[at], g2r.at[at], s2s, s2r.at[n], (me_z, others[1], me_t))
         sent[2, n].start()
 
     half = Z // 2
@@ -283,22 +293,27 @@
     z_out = jnp.clip(jnp.where(low, me_z - 1, me_z + 1), 0, Z - 1)
     Z_INNER, Z_OUTER = 0, 1
 
-    def hop(n, src, slot, target):
-        at = view(n)
-        return remote(src.at[at], gzr.at[(slot,) + at], s3s.at[slot, n], s3r.at[slot, n], (target, me_s, me_t))
+    def hop(n, src, send, slot, target):
+        at = view(n)
+        return remote(src.at[at], gzr.at[(slot,) + at], s3s.at[send], s3r.at[slot, n], (target, me_s, me_t))
 
     def to_inner(n):
-        return hop(n, gz, Z_OUTER, z_in)
+        return hop(n, gz, 0, Z_OUTER, z_in)
 
     def across(n):
-        return hop(n, gz, Z_INNER, z_in)
+        return hop(n, gz, 0, Z_INNER, z_in)
 
     def to_outer(n):
-        return hop(n, gf, Z_INNER, z_out)
+        return hop(n, gf, 1, Z_INNER, z_out)
+
+    def result(n, value):
+        at = view(n)
+        sums[at] = value.astype(F32) * scale
+        pltpu.make_async_copy(sums.at[at], sums_out.at[at], rsem).start()
 
     def step2(n):
         at = view(n)
-        sent[2, n].wait()
+        sent[2, n].wait_recv()
         total = gsend[(me_c, me_u) + at].astype(F32) + g1[(me_u,) + at].astype(F32)
         total = total + g2r[at].astype(F32)
         gzf[at] = total
@@ -326,6 +341,7 @@
             value = (gz[at].astype(F32) + gzr[(Z_INNER,) + at].astype(F32)).astype(BF16)
             gf[at] = value
             to_outer(n).start()
+            result(n, value)
 
     def step5(n):
         at = view(n)
@@ -333,17 +349,23 @@
         @pl.when(is_end)
         def _():
             across(n).wait_recv()
-            gf[at] = gzr[(Z_INNER,) + at]
-
-    def finish(n):
+            result(n, gzr[(Z_INNER,) + at])
+
+    def finish():
+        remote(og, opad.at[pl.ds(Pl, F * Pl), my_cols], osend, orecv.at[0], mate).wait_send()
+        part = hid.at[pl.ds(0, (F - U) * Pl), my_cols]
+        remote(part, part, xsend, xrecv.at[0], x_mate).wait_send()
+        remote(slices(Z - 1), slices(Z - 1), wzsend, wzrecv.at[0], (z_in, me_s, me_t)).wait_send()
+        remote(slices(Z), slices(Z), wxsend, wxrecv.at[0], x_mate).wait_send()
+        remote(gsend.at[1 - me_c], g1, s1s, s1r.at[0], near).wait_send()
+        remote(g2s, g2r, s2s, s2r.at[0], (me_z, others[1], me_t)).wait_send()
+        remote(gz, gzr.at[Z_INNER], s3s.at[0], s3r.at[0, 0], (z_in, me_s, me_t)).wait_send()
+
         @pl.when(is_inner)
         def _():
-            across(n).wait_send()
-            to_outer(n).wait_send()
-
-        @pl.when(is_end)
-        def _():
-            to_inner(n).wait_send()
+            remote(gf, gzr.at[Z_INNER], s3s.at[1], s3r.at[0, 0], (z_out, me_s, me_t)).wait_send()
+
+        pltpu.make_async_copy(sums, sums_out, rsem).wait()
 
     def gradient(tap):
         if tap < KT:
@@ -360,44 +382,34 @@
     for tap in range(KT):
         with scope(f"g_{tap}"):
             gradient(tap)
-    with scope("passlast"):
-        for dz in range(2, Z - 1):
-            pass_on(dz)
     with scope("early0"):
-        step1(early[0])
+        for n in early[:2]:
+            step1(n)
     with scope("hiddenown"):
         for k in range(F - U, F):
             f = frame(k)
             hid[block(f), my_cols] = hidden(twv, f * Pl, Pl)
     with scope("early"):
-        for n in early[1:]:
+        for n in early[2:]:
             step1(n)
     with scope("wwait"):
-        for copy in wcopies:
-            copy.wait()
-        for copy in wzcopies:
-            copy.wait_send()
+        remote(slices(2 * Z), slices(2 * Z), wcsem.at[0], wcsem.at[1], near).wait()
     with scope("hiddenrest"):
         hid[:, mate_cols] = hidden(twx, 0, F * Pl)
     to_sib = remote(hid.at[block(sib)], hs.at[1, block(me_s, WS)], bsem.at[0], bsem.at[1], near)
     to_sib.start()
-    ycopies = []
     with scope("relay"):
         for slot in range(2):
             source = others[1 + slot]
             remote(
-                landing(source), landing(source), xsend.at[slot], xrecv.at[slot], (me_z, source, me_t)
+                landing(source), landing(source), xsend, xrecv.at[slot], (me_z, source, me_t)
             ).wait_recv()
-            copy = remote(landing(source), landing(source), ysend.at[slot], yrecv.at[slot], mate)
-            copy.start()
-            ycopies.append(copy)
+            remote(landing(source), landing(source), ysem.at[0], ysem.at[1], mate).start()
 
     def arrive():
         to_sib.wait()
-        for copy in ycopies:
-            copy.wait()
-        for copy in xcopies:
-            copy.wait_send()
+        part = hs.at[1, pl.ds(pl.multiple_of(WS + far * Pl, 16), 2 * Pl), my_cols]
+        remote(part, part, ysem.at[0], ysem.at[1], mate).wait()
         hs[1, block(me_s, WS), :] = hid[block(me_s), :]
 
     tile = 4 * WS
@@ -412,17 +424,22 @@
                 value = hwide[pl.ds(8 + r - b, tile), :]
                 hs[b + 1, pl.ds(WS + r, tile), :] = jnp.where(keep, value, 0.0).astype(BF16)
 
-    images = swv.shape[0]
-
-    def image(tap):
+    images = 2 * swv.shape[0]
+    image_out = pltpu.make_async_copy(ig, ig_out, isem)
+
+    def image(n):
+        tap, at = n // 2, (n % 2) * (HW // 2)
         row, col = tap // 3, tap % 3
-        term = nt(hs[col, pl.ds((2 - row) * WS, HW), :], swv[tap])
+        rows = pl.ds(at, HW // 2)
+        term = nt(hs[col, pl.ds((2 - row) * WS + at, HW // 2), :], swv[tap])
         if tap == 0:
-            acc[...] = term
-        elif tap < images - 1:
-            acc[...] += term
+            acc[rows, :] = term
+        elif n < images - 2:
+            acc[rows, :] += term
         else:
-            ig[...] = (acc[...] + term).astype(BF16)
+            ig[rows, :] = (acc[rows, :] + term).astype(BF16)
+        if n == images - 1:
+            image_out.start()
 
     steps = {1: step1, 2: step2, 3: step3, 4: step4, 5: step5, "g": gradient, "i": image}
     for kind, n in order(chunks, KT, images, Cl):
@@ -434,8 +451,8 @@
             else:
                 steps[kind](n)
     with scope("fin"):
-        for n in range(len(chunks)):
-            finish(n)
+        finish()
+        image_out.wait()
 
 
 def fused(sizes, latents, saved_input, out_grad, temporal_weight, spatial_weight):
@@ -447,9 +464,9 @@
     Cs = C // S
     U = S // 2
     scale = 1.0 / math.sqrt(Z * F * HS * WS)
-    chunks = pieces_of(list(range(taps)), [1] * KT + PARTS, Cl)
+    chunks = pieces_of(list(range(KT)) + [KT + tap for tap in FIRST], PARTS, Cl)
     N = len(chunks)
-    dims = (S, T, Z, F, Pl, Cl, Cs, chunks, KT)
+    dims = (S, T, Z, F, Pl, Cl, Cs, scale, chunks, KT)
     V = pltpu.VMEM
     D = pltpu.SemaphoreType.DMA
     hbm = pl.BlockSpec(memory_space=pltpu.HBM)
@@ -458,21 +475,21 @@
         functools.partial(kernel, dims),
         out_shape=(
             jax.ShapeDtypeStruct((HW, Cl), BF16),
-            jax.ShapeDtypeStruct((taps, Cl, Cs), BF16),
+            jax.ShapeDtypeStruct((taps, Cl, Cs), F32),
         ),
         in_specs=[hbm] * 5,
-        out_specs=(vmem,) * 2,
+        out_specs=(pl.BlockSpec(memory_space=pl.ANY),) * 2,
         scratch_shapes=[
             V((F * Pl, Cl), BF16), V((KT, Cl, C), BF16), V((KT, Cl, C), BF16), V((taps - KT, Cl, C), BF16),
             V(((F + 2) * Pl, C), BF16), V((F * Pl, C), BF16), V((Cl, F * Pl), BF16),
             V((F, Pl + 4 * WS, Cl), BF16), V((Pl + 4 * WS, Cl), F32), V((taps - KT, Cl, F * Pl), BF16),
             V((HW + 16, C), F32), V((3, HW + 2 * WS, C), BF16), V((HW, Cl), F32),
+            V((HW, Cl), BF16), V((taps, Cl, Cs), BF16), V((taps, Cl, Cs), F32),
             V((2, U, taps, Cl, Cs), BF16), V((U, taps, Cl, Cs), BF16), V((taps, Cl, Cs), BF16),
             V((taps, Cl, Cs), BF16), V((taps, Cl, Cs), BF16), V((taps, Cl, Cs), F32), V((2, taps, Cl, Cs), BF16),
-            D((4,)), D((F,)), D((F,)), D((F,)), D((U,)), D((U,)), D((2,)), D((2,)), D((2,)),
-            D((3,)), D((3,)), D((2,)), D((Z - 1,)), D((Z - 1,)), D((Z,)), D((Z,)),
-            D((N,)), D((N,)), D((N,)), D((N,)),
-            D((2, N)), D((2, N)),
+            D((4,)), D(()), D((F,)), D(()), D(()), D((2,)), D((2,)), D((2,)), D((2,)),
+            D((2,)), D(()), D((Z - 1,)), D(()), D((Z,)), D((2,)),
+            D(()), D((N,)), D(()), D((N,)), D((2,)), D((2, N)), D(()), D(()),
         ],
         compiler_params=pltpu.CompilerParams(
             collective_id=0, has_side_effects=True, vmem_limit_bytes=40 * 2**20
@@ -485,10 +502,19 @@
         )
     ))
 
-    def finish(ig_ref, sums_ref, ig_out, tg_out, sg_out):
-        ig_out[...] = ig_ref[...]
-        tg_out[...] = sums_ref[:KT].astype(F32) * scale
-        sg_out[...] = sums_ref[KT:].astype(F32) * scale
+    def finish(ig_ref, sums_ref, ig_out, tg_out, sg_out, sem):
+        half = (taps - KT) // 2
+        pairs = (
+            (sums_ref.at[pl.ds(KT, half)], sg_out.at[pl.ds(0, half)]),
+            (sums_ref.at[pl.ds(KT + half, taps - KT - half)], sg_out.at[pl.ds(half, taps - KT - half)]),
+            (sums_ref.at[pl.ds(0, KT)], tg_out),
+            (ig_ref, ig_out),
+        )
+        copies = [pltpu.make_async_copy(src, dst, sem.at[n]) for n, (src, dst) in enumerate(pairs)]
+        for copy in copies:
+            copy.start()
+        for copy in copies:
+            copy.wait()
 
     ig, tg, sg = pl.pallas_call(
         finish,
@@ -498,7 +524,8 @@
             jax.ShapeDtypeStruct((taps - KT, Cl, Cs), F32),
         ),
         in_specs=[vmem] * 2,
-        out_specs=(vmem,) * 3,
+        out_specs=(hbm,) * 3,
+        scratch_shapes=[D((4,))],
         compiler_params=pltpu.CompilerParams(vmem_limit_bytes=16 * 2**20),
     )(ig, sums)
     return ig.reshape(latents.shape), tg, sg
@@ -553,7 +580,10 @@
     return input_grad, temporal_grad, spatial_grad
 
 
-PARTS = [2, 1, 1, 1, 1, 1, 1, 2, 2]
+PARTS = [2, 1, 1, 1, 1, 1, 1, 1, 1, 1, 2, 4]
+HOP = 2.1
+START = -2.4
+FIRST = [4, 3, 5, 0, 1, 2, 6, 7, 8]
 
 
 def solution(mesh):

time: 57.1 us -> 55.1 us (0.965)
  Pallas kernels: 56.3 us -> 54.3 us
    pallas_call x1, Pallas kernels: 54.9 us -> 53 us  [fused(): pl.pallas_call(functools.partial(kernel, dims), out_shape=(jax.ShapeDtype...]
where the time goes in v3:
time: 55.1 us; the launch traced here: 55 us
  Pallas kernels  54.3 us (99%)
  between operations  0.64 us (1%)
    pallas_call x1, Pallas kernels, fused(): pl.pallas_call(functools.partial(kernel, dims), out_shape=(jax.ShapeDtype...  53 us
    pallas_call x1, Pallas kernels, fused(): pl.pallas_call(finish, out_shape=(jax.ShapeDtypeStruct((HW, Cl), BF16), j...  1.35 us

profile of v3, /device:TPU:0, one launch (start us, length us, event | category | flops | bytes accessed | tf_op | source)
XLA Modules:
  0.0 55.0 jit_solution(10116840517928335538)
XLA Ops:
  0.6 53.0 %shard_map.76 = (bf16[1024,256]{1,0:T(8,128)(2,1)S(1)}, f32[12,256,128]{2,1,0:T(8,128)S(1)}) custom-call(bf16[1024,256]{1,0:T(8,128)(2,1)} %bitcast.4, bf16[1024,256]{1,0:T(8,128)(2,1)} %bitcast.5, bf16[1024,256]{1,0:T(8,128)(2,1)} %bitcast.6, bf16[3,256,512]{2,1,0:T(8,128)(2,1)} %tw.1, bf16[9,256,512]{2,1,0:T(8,128)(2,1)} %sw.1), custom_call_target="tpu_custom_call" | custom-call | tf_op jit(solution)/shard_map/pallas_call | solution.py:474
  53.6 1.3 %shard_map.77 = (bf16[1024,256]{1,0:T(8,128)(2,1)}, f32[3,256,128]{2,1,0:T(8,128)}, f32[9,256,128]{2,1,0:T(8,128)}) custom-call(bf16[1024,256]{1,0:T(8,128)(2,1)S(1)} %get-tuple-element.8.ig_ref, f32[12,256,128]{2,1,0:T(8,128)S(1)} %get-tuple-element.9.sums_ref), custom_call_target="tpu_custom_call" | custom-call | tf_op jit(solution)/shard_map/pallas_call | solution.py:519

commit v4 on v3

--- a/solution.py
+++ b/solution.py
@@ -35,56 +35,76 @@
     return [(tap, part * (rows // n), rows // n) for tap, n in zip(taps, parts) for part in range(n)]
 
 
-def order(chunks, first, images, rows):
+def order(chunks, lead, early_taps, images, rows):
     hop, core_hop, link, core = HOP, 0.65, 1.39, 0.44
-    arrival = 8.0
-    now, free = START, {"core": 0.0, "x": START, "z": 0.0, "across": 0.0, "back": 0.0}
+    now, free = START, {"core": 0.0, "x": START, "z": LEAD, "across": 0.0, "back": 0.0}
     pending, out = {}, []
 
-    def send(name, n, step):
-        part = chunks[n][2] / rows
+    def send(name, part, key, step=None):
         free[name] = max(free[name], now) + (core if name == "core" else link) * part
-        pending[step, n] = free[name] + (core_hop if name == "core" else hop)
+        pending[key] = free[name] + (core_hop if name == "core" else hop) + LATE.get(key[0], 0.0)
 
     taps = list(dict.fromkeys(tap for tap, _, _ in chunks))
-    late, filler = taps[first:], ["h", "s"] + list(range(images))
+    late = taps[early_taps:]
+    filler = ["a"] + list(range(images // 2)) + ["h"] + list(range(images // 2, images))
     for n, chunk in enumerate(chunks):
-        if chunk[0] in taps[:first]:
-            send("x", n, 2)
+        if chunk[0] not in late:
+            send("x", chunk[2] / rows, (2, n))
+    now = LEAD
+    for n in range(lead):
+        send("z", 2 / lead, ("B", n))
     now = 0.0
+    gate = {"a": NEAR, "h": 1e9}
+    pending["r", 0], pending["r", 1] = EARLY, EARLY + 1.4
     while pending or late or filler:
-        ready = sorted((at, key) for key, at in pending.items() if at <= now)
+        ready = sorted((at, str(key), key) for key, at in pending.items() if at <= now)
         if ready:
-            at, (step, n) = ready[0]
-            now += 0.06 * chunks[n][2] / rows
+            at, _, (step, n) = ready[0]
             del pending[step, n]
             out.append((step, n))
-            if step < 5:
-                send(("core", "x", "z", "across", "back")[step], n, step + 1)
+            if step == "r":
+                now += 0.05
+                gate["h"] = now + 2.5 * link + hop if n else gate["h"]
+            elif isinstance(step, str):
+                now += 0.05
+                if step == "B":
+                    send("across", 2 / lead, ("C", n))
+                elif step == "C":
+                    send("back", 2 / lead, ("D", n))
+                elif step == "D":
+                    send("x", 1 / lead, ("E", n))
+            else:
+                part = chunks[n][2] / rows
+                now += 0.06 * part
+                if step < 5:
+                    send(("core", "x", "z", "across", "back")[step], part, (step + 1, n))
             continue
         soon = min(pending.values()) if pending else 1e9
         if late:
             tap = late.pop(0)
             out.append(("g", tap))
-            now += 0.7 if len(taps) - first - len(late) <= 3 else 0.45
+            now += 0.7 if len(taps) - early_taps - len(late) <= 3 else 0.45
             for n, chunk in enumerate(chunks):
                 if chunk[0] == tap:
-                    send("core", n, 1)
-        elif filler and now >= arrival and (soon > now + 0.25 or not pending):
+                    send("core", chunk[2] / rows, (1, n))
+            continue
+        at = gate.get(filler[0], 0.0) if filler else 0.0
+        waits = now < at
+        if filler and not waits and (soon > now + SLACK or not pending):
             kind = filler.pop(0)
             out.append((kind, 0) if isinstance(kind, str) else ("i", kind))
-            now += 0.1 if kind == "h" else 0.55 if kind == "s" else 0.3
+            now += 0.3
         else:
-            now = max(now, soon if not filler or now >= arrival else min(soon, arrival))
+            now = max(now, min(soon, at) if waits else soon)
     return out
 
 
 def kernel(
     dims, lat, sav, og, tw, sw, ig_out, sums_out,
-    savv, twv, twx, swv, opad, hid, savt, latl, lwide, latt, hwide, hs, acc, ig, gf, sums,
-    gsend, g1, g2s, g2r, gz, gzf, gzr,
+    savv, twv, twx, swv, opad, hid, savt, most, latl, lwide, latt, hs, acc, ig, gf, sums,
+    gsend, g1, g2s, g2r, gz, gzf, gzr, qs, qf, qr, qown, qx,
     lsem, osend, orecv, osem, xsend, xrecv, bsem, ysem, lxsem, wysem, wzsend, wzrecv, wxsend, wxrecv, wcsem,
-    s1s, s1r, s2s, s2r, s3s, s3r, isem, rsem,
+    s1s, s1r, s2s, s2r, s3s, s3r, isem, rsem, entered, qcore, qsem, qrecv, qxrecv,
 ):
     S, T, Z, F, Pl, Cl, Cs, scale, chunks, KT = dims
     U = S // 2
@@ -133,14 +153,23 @@
     with scope("barrier"):
         barrier = pltpu.get_barrier_semaphore()
         peers = [mate, near, (me_z, others[1], me_t), (me_z, others[2], me_t)]
-        count = len(peers) + Z - 1
+        first, last = me_z == 0, me_z == Z - 1
+        count = len(peers) + jnp.where(jnp.logical_or(first, last), 1, 2)
         for peer in peers:
             pl.semaphore_signal(barrier, inc=1, device_id=peer, device_id_type=MESH)
-        for dz in range(1, Z):
-            pl.semaphore_signal(
-                barrier, inc=1, device_id=(lax.rem(me_z + dz, Z), me_s, me_t), device_id_type=MESH
-            )
+
+        def tell(semaphore, step, sends):
+            @pl.when(sends)
+            def _():
+                pl.semaphore_signal(
+                    semaphore, inc=1, device_id=(jnp.clip(me_z + step, 0, Z - 1), me_s, me_t), device_id_type=MESH
+                )
+
+        tell(barrier, 1, jnp.logical_not(last))
+        tell(barrier, -1, jnp.logical_not(first))
         pl.semaphore_wait(barrier, count)
+        tell(entered.at[0], 1, me_z == 1)
+        tell(entered.at[1], -1, me_z == Z - 2)
 
     def frame(k):
         return jnp.where(me_u == 0, F - 1 - k, k)
@@ -172,8 +201,6 @@
 
     opad[pl.ds(0, Pl), :] = jnp.zeros((Pl, C), BF16)
     opad[pl.ds((F + 1) * Pl, Pl), :] = jnp.zeros((Pl, C), BF16)
-    hwide[pl.ds(0, 8), :] = jnp.zeros((8, C), F32)
-    hwide[pl.ds(8 + HW, 8), :] = jnp.zeros((8, C), F32)
     for b in range(3):
         hs[b, pl.ds(0, WS), :] = jnp.zeros((WS, C), BF16)
         hs[b, pl.ds(WS + HW, WS), :] = jnp.zeros((WS, C), BF16)
@@ -181,7 +208,9 @@
         own_og.wait()
         for copy in loads:
             copy.wait()
-    savt[...] = savv[...].T
+    savt[:, pl.ds(0, Pl)] = jnp.zeros((Cl, Pl), BF16)
+    savt[:, pl.ds((F + 1) * Pl, Pl)] = jnp.zeros((Cl, Pl), BF16)
+    savt[:, pl.ds(Pl, F * Pl)] = savv[...].T
 
     def pass_x(n):
         piece = slice_of(me_u, me_c, lax.rem(me_z + Z - n, Z))
@@ -198,8 +227,17 @@
         remote(piece, piece, wxsend, wxrecv.at[n], x_mate).wait_recv()
         remote(piece, piece, wcsem.at[0], wcsem.at[1], near).start()
 
+    def hear(semaphore, step, hears, sends):
+        @pl.when(hears)
+        def _():
+            pl.semaphore_wait(semaphore, 1)
+
+        tell(semaphore, step, sends)
+
     with scope("wy"):
         wy.wait()
+        hear(entered.at[0], 1, me_z >= 2, jnp.logical_and(me_z >= 2, me_z < Z - 1))
+        hear(entered.at[1], -1, me_z <= Z - 3, jnp.logical_and(me_z <= Z - 3, me_z > 0))
     for dz in (1, Z - 1, 2):
         piece = slice_of(me_u, me_c, me_z)
         remote(piece, piece, wzsend, wzrecv.at[dz - 1], (lax.rem(me_z + dz, Z), me_s, me_t)).start()
@@ -227,8 +265,18 @@
             for row in range(3):
                 latt[3 * row + b, :, pl.ds(f * Pl, Pl)] = value[row * WS : row * WS + Pl].T
 
-    def landing(n):
-        return hs.at[1, block(n, WS), my_cols]
+    def landing(n, part):
+        at = pl.multiple_of(WS + n * Pl + part * (Pl // 2), 16)
+        return hs.at[1, pl.ds(at, Pl // 2), my_cols]
+
+    def send_block(k, parts=(0, 1)):
+        f = frame(k)
+        for part in parts:
+            rows = pl.ds(pl.multiple_of(f * Pl + part * (Pl // 2), 16), Pl // 2)
+            remote(
+                hid.at[rows, my_cols], landing(me_s, part),
+                xsend, xrecv.at[part, lax.rem(f + me_c, 2)], (me_z, f, me_t),
+            ).start()
 
     def hidden(weights, at, size):
         total = None
@@ -248,22 +296,30 @@
 
     for k in range(F - U):
         f = frame(k)
-        with scope(f"lshift{k}"):
-            for part_f in range(k * U, (k + 1) * U):
-                latents_of(part_f)
         if k == 0:
+            with scope("lshift0"):
+                for part_f in range(U):
+                    latents_of(part_f)
             with scope("passz2"):
                 pass_z(2)
         take(k + 2)
         with scope(f"hidden{k}"):
             hid[block(f), my_cols] = hidden(twv, f * Pl, Pl)
-        copy = remote(
-            hid.at[block(f), my_cols], landing(me_s), xsend, xrecv.at[lax.rem(f + me_c, 2)], (me_z, f, me_t)
-        )
-        copy.start()
-        with scope(f"pass{k}"):
-            for n in ((0, 1), (Z - 1, 2))[k]:
-                pass_core(n)
+        send_block(k)
+        if k == 0:
+            with scope("lshift1"):
+                for part_f in range(U, F):
+                    latents_of(part_f)
+    with scope("passc"):
+        pass_core(0)
+        pass_core(1)
+    base = jnp.where(me_u == 0, U, 1)
+    for tap in range(KT):
+        with scope(f"p_{tap}"):
+            at = pl.multiple_of((base + tap - 1) * Pl, 128)
+            most[tap] = nn(
+                savt[:, pl.ds(at, (F - 1) * Pl)], opad[pl.ds(pl.multiple_of(base * Pl, 16), (F - 1) * Pl), :]
+            )
     take(F)
 
     sent = {}
@@ -354,22 +410,27 @@
     def finish():
         remote(og, opad.at[pl.ds(Pl, F * Pl), my_cols], osend, orecv.at[0], mate).wait_send()
         part = hid.at[pl.ds(0, (F - U) * Pl), my_cols]
-        remote(part, part, xsend, xrecv.at[0], x_mate).wait_send()
+        remote(part, part, xsend, xrecv.at[0, 0], x_mate).wait_send()
         remote(slices(Z - 1), slices(Z - 1), wzsend, wzrecv.at[0], (z_in, me_s, me_t)).wait_send()
         remote(slices(Z), slices(Z), wxsend, wxrecv.at[0], x_mate).wait_send()
         remote(gsend.at[1 - me_c], g1, s1s, s1r.at[0], near).wait_send()
         remote(g2s, g2r, s2s, s2r.at[0], (me_z, others[1], me_t)).wait_send()
-        remote(gz, gzr.at[Z_INNER], s3s.at[0], s3r.at[0, 0], (z_in, me_s, me_t)).wait_send()
+        rest = pl.ds(1, gz.shape[0] - 1)
+        remote(gz.at[rest], gzr.at[Z_INNER, rest], s3s.at[0], s3r.at[0, 0], (z_in, me_s, me_t)).wait_send()
+        remote(qs, qr.at[Z_INNER], qsem.at[0], qrecv.at[0, 0], (z_in, me_s, me_t)).wait_send()
 
         @pl.when(is_inner)
         def _():
-            remote(gf, gzr.at[Z_INNER], s3s.at[1], s3r.at[0, 0], (z_out, me_s, me_t)).wait_send()
+            remote(gf.at[rest], gzr.at[Z_INNER, rest], s3s.at[1], s3r.at[0, 0], (z_out, me_s, me_t)).wait_send()
+            remote(qf, qr.at[Z_INNER], qsem.at[1], qrecv.at[0, 0], (z_out, me_s, me_t)).wait_send()
 
         pltpu.make_async_copy(sums, sums_out, rsem).wait()
 
     def gradient(tap):
         if tap < KT:
-            part = nn(savt[...], opad[pl.ds((KT - 1 - tap) * Pl, F * Pl), :])
+            f = frame(F - 1)
+            at = pl.multiple_of((f + tap) * Pl, 128)
+            part = most[tap] + nn(savt[:, pl.ds(at, Pl)], opad[block(f, Pl), :])
         else:
             part = nn(latt[tap - KT], hid[...])
         for s in range(S):
@@ -377,20 +438,97 @@
         for n, chunk in enumerate(chunks):
             if chunk[0] == tap:
                 start1(n)
+        if tap == 0:
+            for n in range(LEADS):
+                rows = lead_rows(n)
+                remote(gsend.at[1 - me_c, :, 0, rows], g1.at[:, 0, rows], s1s, qcore.at[n], near).start()
+
+    piece_rows = Cl // LEADS
+
+    def lead_rows(n):
+        return pl.ds(n * piece_rows, piece_rows)
+
+    def lead_hop(n, src, send, slot, target):
+        return remote(
+            src.at[:, lead_rows(n)], qr.at[slot, :, lead_rows(n)], qsem.at[send], qrecv.at[slot, n],
+            (target, me_s, me_t),
+        )
+
+    def lead_a(n):
+        rows = lead_rows(n)
+        remote(gsend.at[1 - me_c, :, 0, rows], g1.at[:, 0, rows], s1s, qcore.at[n], near).wait_recv()
+        total = gsend[me_c, :, 0, rows].astype(F32) + g1[:, 0, rows].astype(F32)
+
+        @pl.when(is_end)
+        def _():
+            qs[:, rows] = total.astype(BF16)
+            lead_hop(n, qs, 0, Z_OUTER, z_in).start()
+
+        @pl.when(is_inner)
+        def _():
+            qown[:, rows] = total
+
+    def lead_b(n):
+        rows = lead_rows(n)
+
+        @pl.when(is_inner)
+        def _():
+            lead_hop(n, qs, 0, Z_OUTER, z_in).wait_recv()
+            qs[:, rows] = (qown[:, rows] + qr[Z_OUTER, :, rows].astype(F32)).astype(BF16)
+            lead_hop(n, qs, 0, Z_INNER, z_in).start()
+
+    def lead_x(n, src):
+        return remote(src.at[lead_rows(n)], qx.at[lead_rows(n)], s2s, qxrecv.at[n], x_mate)
+
+    def lead_c(n):
+        rows = lead_rows(n)
+
+        @pl.when(is_inner)
+        def _():
+            lead_hop(n, qs, 0, Z_INNER, z_in).wait_recv()
+            qf[:, rows] = (qs[:, rows].astype(F32) + qr[Z_INNER, :, rows].astype(F32)).astype(BF16)
+            lead_hop(n, qf, 1, Z_INNER, z_out).start()
+            lead_x(n, qf.at[1 - me_u]).start()
+
+    def lead_d(n):
+        @pl.when(is_end)
+        def _():
+            lead_hop(n, qs, 0, Z_INNER, z_in).wait_recv()
+            lead_x(n, qr.at[Z_INNER, 1 - me_u]).start()
+
+    def lead_e(n):
+        rows = lead_rows(n)
+        lead_x(n, qf.at[1 - me_u]).wait_recv()
+
+        def done(mine):
+            sums[0, rows] = (mine.astype(F32) + qx[rows].astype(F32)) * scale
+            pltpu.make_async_copy(sums.at[0, rows], sums_out.at[0, rows], rsem).start()
+
+        @pl.when(is_inner)
+        def _():
+            done(qf[me_u, rows])
+
+        @pl.when(is_end)
+        def _():
+            done(qr[Z_INNER, me_u, rows])
 
     early = [n for n, chunk in enumerate(chunks) if chunk[0] < KT]
     for tap in range(KT):
         with scope(f"g_{tap}"):
             gradient(tap)
+        if tap == 0:
+            with scope("passd"):
+                pass_core(Z - 1)
+                pass_core(2)
     with scope("early0"):
-        for n in early[:2]:
-            step1(n)
+        for n in range(LEADS):
+            lead_a(n)
     with scope("hiddenown"):
         for k in range(F - U, F):
             f = frame(k)
             hid[block(f), my_cols] = hidden(twv, f * Pl, Pl)
     with scope("early"):
-        for n in early[2:]:
+        for n in early:
             step1(n)
     with scope("wwait"):
         remote(slices(2 * Z), slices(2 * Z), wcsem.at[0], wcsem.at[1], near).wait()
@@ -398,56 +536,65 @@
         hid[:, mate_cols] = hidden(twx, 0, F * Pl)
     to_sib = remote(hid.at[block(sib)], hs.at[1, block(me_s, WS)], bsem.at[0], bsem.at[1], near)
     to_sib.start()
-    with scope("relay"):
+    def relay(part):
         for slot in range(2):
-            source = others[1 + slot]
-            remote(
-                landing(source), landing(source), xsend, xrecv.at[slot], (me_z, source, me_t)
-            ).wait_recv()
-            remote(landing(source), landing(source), ysem.at[0], ysem.at[1], mate).start()
-
-    def arrive():
+            piece = landing(others[1 + slot], part)
+            remote(piece, piece, xsend, xrecv.at[part, slot], (me_z, others[1 + slot], me_t)).wait_recv()
+            remote(piece, piece, ysem.at[0], ysem.at[1], mate).start()
+
+    def arrive_near():
         to_sib.wait()
+        hs[1, block(me_s, WS), :] = hid[block(me_s), :]
+        shift(me_u * (HW // 2))
+
+    def arrive_far():
         part = hs.at[1, pl.ds(pl.multiple_of(WS + far * Pl, 16), 2 * Pl), my_cols]
         remote(part, part, ysem.at[0], ysem.at[1], mate).wait()
-        hs[1, block(me_s, WS), :] = hid[block(me_s), :]
+        shift((1 - me_u) * (HW // 2))
 
     tile = 4 * WS
 
-    def shift():
-        for r in range(0, HW, tile):
-            hwide[pl.ds(8 + r, tile), :] = hs[1, pl.ds(WS + r, tile), :].astype(F32)
+    def shift(base):
         column = lax.rem(lax.broadcasted_iota(jnp.int32, (tile, C), 0), WS)
-        for b in (-1, 1):
-            keep = column != (0 if b == 1 else WS - 1)
-            for r in range(0, HW, tile):
-                value = hwide[pl.ds(8 + r - b, tile), :]
-                hs[b + 1, pl.ds(WS + r, tile), :] = jnp.where(keep, value, 0.0).astype(BF16)
+        for r in range(0, HW // 2, tile):
+            rows = pl.ds(pl.multiple_of(base + WS + r, WS), tile)
+            value = hs[1, rows, :].astype(F32)
+            for b in (-1, 1):
+                keep = column != (0 if b == 1 else WS - 1)
+                moved = pltpu.roll(value, 1 if b == 1 else tile - 1, 0)
+                hs[b + 1, rows, :] = jnp.where(keep, moved, 0.0).astype(BF16)
 
     images = 2 * swv.shape[0]
     image_out = pltpu.make_async_copy(ig, ig_out, isem)
+    near_rows, far_rows = HW // 2 - WS, HW // 2 + WS
+    near_at = me_u * far_rows
+    far_at = (1 - me_u) * near_rows
 
     def image(n):
-        tap, at = n // 2, (n % 2) * (HW // 2)
+        tap = n % (images // 2)
         row, col = tap // 3, tap % 3
-        rows = pl.ds(at, HW // 2)
-        term = nt(hs[col, pl.ds((2 - row) * WS + at, HW // 2), :], swv[tap])
+        at, size = (near_at, near_rows) if n < images // 2 else (far_at, far_rows)
+        rows = pl.ds(pl.multiple_of(at, WS), size)
+        term = nt(hs[col, pl.ds(pl.multiple_of(at + (2 - row) * WS, WS), size), :], swv[tap])
         if tap == 0:
             acc[rows, :] = term
-        elif n < images - 2:
+        elif tap < images // 2 - 1:
             acc[rows, :] += term
         else:
             ig[rows, :] = (acc[rows, :] + term).astype(BF16)
         if n == images - 1:
             image_out.start()
 
-    steps = {1: step1, 2: step2, 3: step3, 4: step4, 5: step5, "g": gradient, "i": image}
-    for kind, n in order(chunks, KT, images, Cl):
+    steps = {"B": lead_b, "C": lead_c, "D": lead_d, "E": lead_e}
+    steps |= {1: step1, 2: step2, 3: step3, 4: step4, 5: step5, "g": gradient, "i": image}
+    for kind, n in order(chunks, LEADS, KT - 1, images, Cl):
         with scope(f"{kind}_{n}"):
-            if kind == "h":
-                arrive()
-            elif kind == "s":
-                shift()
+            if kind == "r":
+                relay(n)
+            elif kind == "a":
+                arrive_near()
+            elif kind == "h":
+                arrive_far()
             else:
                 steps[kind](n)
     with scope("fin"):
@@ -464,7 +611,7 @@
     Cs = C // S
     U = S // 2
     scale = 1.0 / math.sqrt(Z * F * HS * WS)
-    chunks = pieces_of(list(range(KT)) + [KT + tap for tap in FIRST], PARTS, Cl)
+    chunks = pieces_of(list(range(1, KT)) + [KT + tap for tap in FIRST], PARTS, Cl)
     N = len(chunks)
     dims = (S, T, Z, F, Pl, Cl, Cs, scale, chunks, KT)
     V = pltpu.VMEM
@@ -481,18 +628,20 @@
         out_specs=(pl.BlockSpec(memory_space=pl.ANY),) * 2,
         scratch_shapes=[
             V((F * Pl, Cl), BF16), V((KT, Cl, C), BF16), V((KT, Cl, C), BF16), V((taps - KT, Cl, C), BF16),
-            V(((F + 2) * Pl, C), BF16), V((F * Pl, C), BF16), V((Cl, F * Pl), BF16),
+            V(((F + 2) * Pl, C), BF16), V((F * Pl, C), BF16), V((Cl, (F + 2) * Pl), BF16), V((KT, Cl, C), F32),
             V((F, Pl + 4 * WS, Cl), BF16), V((Pl + 4 * WS, Cl), F32), V((taps - KT, Cl, F * Pl), BF16),
-            V((HW + 16, C), F32), V((3, HW + 2 * WS, C), BF16), V((HW, Cl), F32),
+            V((3, HW + 2 * WS, C), BF16), V((HW, Cl), F32),
             V((HW, Cl), BF16), V((taps, Cl, Cs), BF16), V((taps, Cl, Cs), F32),
             V((2, U, taps, Cl, Cs), BF16), V((U, taps, Cl, Cs), BF16), V((taps, Cl, Cs), BF16),
             V((taps, Cl, Cs), BF16), V((taps, Cl, Cs), BF16), V((taps, Cl, Cs), F32), V((2, taps, Cl, Cs), BF16),
-            D((4,)), D(()), D((F,)), D(()), D(()), D((2,)), D((2,)), D((2,)), D((2,)),
+            V((U, Cl, Cs), BF16), V((U, Cl, Cs), BF16), V((2, U, Cl, Cs), BF16), V((U, Cl, Cs), F32), V((Cl, Cs), BF16),
+            D((4,)), D(()), D((F,)), D(()), D(()), D((2, 2)), D((2,)), D((2,)), D((2,)),
             D((2,)), D(()), D((Z - 1,)), D(()), D((Z,)), D((2,)),
-            D(()), D((N,)), D(()), D((N,)), D((2,)), D((2, N)), D(()), D(()),
+            D(()), D((N,)), D(()), D((N,)), D((2,)), D((2, N)), D(()), D(()), pltpu.SemaphoreType.REGULAR((2,)),
+            D((LEADS,)), D((2,)), D((2, LEADS)), D((LEADS,)),
         ],
         compiler_params=pltpu.CompilerParams(
-            collective_id=0, has_side_effects=True, vmem_limit_bytes=40 * 2**20
+            collective_id=0, has_side_effects=True, vmem_limit_bytes=44 * 2**20
         ),
     )(*(
         pltpu.with_memory_space_constraint(value, pltpu.HBM)
@@ -580,9 +729,15 @@
     return input_grad, temporal_grad, spatial_grad
 
 
-PARTS = [2, 1, 1, 1, 1, 1, 1, 1, 1, 1, 2, 4]
+PARTS = [4, 4, 2, 2, 2, 2, 2, 2, 2, 2, 4]
 HOP = 2.1
-START = -2.4
+START = -1.0
+LEAD = -2.6
+LEADS = 4
+NEAR = 3.0
+EARLY = 1.5
+SLACK = 0.3
+LATE = {5: 3.0, "E": 2.0}
 FIRST = [4, 3, 5, 0, 1, 2, 6, 7, 8]
 
 

time: 55.1 us -> 53.7 us (0.975)
  Pallas kernels: 54.3 us -> 52.9 us
    pallas_call x1, Pallas kernels: 53 us -> 51.6 us  [fused(): pl.pallas_call(functools.partial(kernel, dims), out_shape=(jax.ShapeDtype...]
where the time goes in v4:
time: 53.7 us; the launch traced here: 53.6 us
  Pallas kernels  52.9 us (99%)
  between operations  0.64 us (1%)
    pallas_call x1, Pallas kernels, fused(): pl.pallas_call(functools.partial(kernel, dims), out_shape=(jax.ShapeDtype...  51.6 us
    pallas_call x1, Pallas kernels, fused(): pl.pallas_call(finish, out_shape=(jax.ShapeDtypeStruct((HW, Cl), BF16), j...  1.35 us

profile of v4, /device:TPU:0, one launch (start us, length us, event | category | flops | bytes accessed | tf_op | source)
XLA Modules:
  0.0 53.6 jit_solution(6498823683606032386)
XLA Ops:
  0.6 51.6 %shard_map.76 = (bf16[1024,256]{1,0:T(8,128)(2,1)S(1)}, f32[12,256,128]{2,1,0:T(8,128)S(1)}) custom-call(bf16[1024,256]{1,0:T(8,128)(2,1)} %bitcast.4, bf16[1024,256]{1,0:T(8,128)(2,1)} %bitcast.5, bf16[1024,256]{1,0:T(8,128)(2,1)} %bitcast.6, bf16[3,256,512]{2,1,0:T(8,128)(2,1)} %tw.1, bf16[9,256,512]{2,1,0:T(8,128)(2,1)} %sw.1), custom_call_target="tpu_custom_call" | custom-call | tf_op jit(solution)/shard_map/pallas_call | solution.py:621
  52.2 1.3 %shard_map.77 = (bf16[1024,256]{1,0:T(8,128)(2,1)}, f32[3,256,128]{2,1,0:T(8,128)}, f32[9,256,128]{2,1,0:T(8,128)}) custom-call(bf16[1024,256]{1,0:T(8,128)(2,1)S(1)} %get-tuple-element.8.ig_ref, f32[12,256,128]{2,1,0:T(8,128)S(1)} %get-tuple-element.9.sums_ref), custom_call_target="tpu_custom_call" | custom-call | tf_op jit(solution)/shard_map/pallas_call | solution.py:668

commit v5 on v4

--- a/solution.py
+++ b/solution.py
@@ -84,9 +84,10 @@
             tap = late.pop(0)
             out.append(("g", tap))
             now += 0.7 if len(taps) - early_taps - len(late) <= 3 else 0.45
+            free["core"] = max(free["core"], now) + core
             for n, chunk in enumerate(chunks):
                 if chunk[0] == tap:
-                    send("core", chunk[2] / rows, (1, n))
+                    pending[1, n] = free["core"] + core_hop
             continue
         at = gate.get(filler[0], 0.0) if filler else 0.0
         waits = now < at
@@ -328,14 +329,14 @@
         tap, at, rows = chunks[n]
         return tap, pl.ds(at, rows)
 
-    def start1(n):
-        at = view(n)
-        sent[1, n] = remote(gsend.at[(1 - me_c, slice(None)) + at], g1.at[(slice(None),) + at], s1s, s1r.at[n], near)
-        sent[1, n].start()
+    def start1(tap):
+        sent[1, tap] = remote(gsend.at[1 - me_c, :, tap], g1.at[:, tap], s1s, s1r.at[tap], near)
+        sent[1, tap].start()
 
     def step1(n):
         at = view(n)
-        sent[1, n].wait_recv()
+        if (1, chunks[n][0]) in sent:
+            sent.pop((1, chunks[n][0])).wait_recv()
         other = 1 - me_u
         g2s[at] = (gsend[(me_c, other) + at].astype(F32) + g1[(other,) + at].astype(F32)).astype(BF16)
         sent[2, n] = remote(g2s.at[at], g2r.at[at], s2s, s2r.at[n], (me_z, others[1], me_t))
@@ -435,10 +436,9 @@
             part = nn(latt[tap - KT], hid[...])
         for s in range(S):
             gsend[s % 2, s // 2, tap] = part[:, s * Cs : (s + 1) * Cs].astype(BF16)
-        for n, chunk in enumerate(chunks):
-            if chunk[0] == tap:
-                start1(n)
-        if tap == 0:
+        if tap:
+            start1(tap)
+        else:
             for n in range(LEADS):
                 rows = lead_rows(n)
                 remote(gsend.at[1 - me_c, :, 0, rows], g1.at[:, 0, rows], s1s, qcore.at[n], near).start()
@@ -637,7 +637,7 @@
             V((U, Cl, Cs), BF16), V((U, Cl, Cs), BF16), V((2, U, Cl, Cs), BF16), V((U, Cl, Cs), F32), V((Cl, Cs), BF16),
             D((4,)), D(()), D((F,)), D(()), D(()), D((2, 2)), D((2,)), D((2,)), D((2,)),
             D((2,)), D(()), D((Z - 1,)), D(()), D((Z,)), D((2,)),
-            D(()), D((N,)), D(()), D((N,)), D((2,)), D((2, N)), D(()), D(()), pltpu.SemaphoreType.REGULAR((2,)),
+            D(()), D((taps,)), D(()), D((N,)), D((2,)), D((2, N)), D(()), D(()), pltpu.SemaphoreType.REGULAR((2,)),
             D((LEADS,)), D((2,)), D((2, LEADS)), D((LEADS,)),
         ],
         compiler_params=pltpu.CompilerParams(
@@ -731,12 +731,12 @@
 
 PARTS = [4, 4, 2, 2, 2, 2, 2, 2, 2, 2, 4]
 HOP = 2.1
-START = -1.0
+START = -0.6
 LEAD = -2.6
 LEADS = 4
 NEAR = 3.0
 EARLY = 1.5
-SLACK = 0.3
+SLACK = 0.25
 LATE = {5: 3.0, "E": 2.0}
 FIRST = [4, 3, 5, 0, 1, 2, 6, 7, 8]
 

time: 53.7 us -> 53.6 us (level)
  no operation moved by 1% of the time
where the time goes in v5:
time: 53.6 us; the launch traced here: 53.4 us
  Pallas kernels  52.8 us (99%)
  between operations  0.64 us (1%)
    pallas_call x1, Pallas kernels, fused(): pl.pallas_call(functools.partial(kernel, dims), out_shape=(jax.ShapeDtype...  51.5 us
    pallas_call x1, Pallas kernels, fused(): pl.pallas_call(finish, out_shape=(jax.ShapeDtypeStruct((HW, Cl), BF16), j...  1.35 us

profile of v5, /device:TPU:0, one launch (start us, length us, event | category | flops | bytes accessed | tf_op | source)
XLA Modules:
  0.0 53.4 jit_solution(18153659549476610783)
XLA Ops:
  0.6 51.5 %shard_map.76 = (bf16[1024,256]{1,0:T(8,128)(2,1)S(1)}, f32[12,256,128]{2,1,0:T(8,128)S(1)}) custom-call(bf16[1024,256]{1,0:T(8,128)(2,1)} %bitcast.4, bf16[1024,256]{1,0:T(8,128)(2,1)} %bitcast.5, bf16[1024,256]{1,0:T(8,128)(2,1)} %bitcast.6, bf16[3,256,512]{2,1,0:T(8,128)(2,1)} %tw.1, bf16[9,256,512]{2,1,0:T(8,128)(2,1)} %sw.1), custom_call_target="tpu_custom_call" | custom-call | tf_op jit(solution)/shard_map/pallas_call | solution.py:621
  52.1 1.3 %shard_map.77 = (bf16[1024,256]{1,0:T(8,128)(2,1)}, f32[3,256,128]{2,1,0:T(8,128)}, f32[9,256,128]{2,1,0:T(8,128)}) custom-call(bf16[1024,256]{1,0:T(8,128)(2,1)S(1)} %get-tuple-element.8.ig_ref, f32[12,256,128]{2,1,0:T(8,128)S(1)} %get-tuple-element.9.sums_ref), custom_call_target="tpu_custom_call" | custom-call | tf_op jit(solution)/shard_map/pallas_call | solution.py:668

commit v6 on v4

--- a/solution.py
+++ b/solution.py
@@ -731,13 +731,13 @@
 
 PARTS = [4, 4, 2, 2, 2, 2, 2, 2, 2, 2, 4]
 HOP = 2.1
-START = -1.0
+START = -0.7
 LEAD = -2.6
 LEADS = 4
 NEAR = 3.0
 EARLY = 1.5
 SLACK = 0.3
-LATE = {5: 3.0, "E": 2.0}
+LATE = {5: 4.0, "E": 4.0}
 FIRST = [4, 3, 5, 0, 1, 2, 6, 7, 8]
 
 

time: 53.7 us -> 53.7 us (level)
  no operation moved by 1% of the time
where the time goes in v6:
time: 53.7 us; the launch traced here: 53.5 us
  Pallas kernels  52.9 us (99%)
  between operations  0.64 us (1%)
    pallas_call x1, Pallas kernels, fused(): pl.pallas_call(functools.partial(kernel, dims), out_shape=(jax.ShapeDtype...  51.5 us
    pallas_call x1, Pallas kernels, fused(): pl.pallas_call(finish, out_shape=(jax.ShapeDtypeStruct((HW, Cl), BF16), j...  1.35 us

profile of v6, /device:TPU:0, one launch (start us, length us, event | category | flops | bytes accessed | tf_op | source)
XLA Modules:
  0.0 53.5 jit_solution(370419466377057409)
XLA Ops:
  0.6 51.5 %shard_map.76 = (bf16[1024,256]{1,0:T(8,128)(2,1)S(1)}, f32[12,256,128]{2,1,0:T(8,128)S(1)}) custom-call(bf16[1024,256]{1,0:T(8,128)(2,1)} %bitcast.4, bf16[1024,256]{1,0:T(8,128)(2,1)} %bitcast.5, bf16[1024,256]{1,0:T(8,128)(2,1)} %bitcast.6, bf16[3,256,512]{2,1,0:T(8,128)(2,1)} %tw.1, bf16[9,256,512]{2,1,0:T(8,128)(2,1)} %sw.1), custom_call_target="tpu_custom_call" | custom-call | tf_op jit(solution)/shard_map/pallas_call | solution.py:621
  52.2 1.3 %shard_map.77 = (bf16[1024,256]{1,0:T(8,128)(2,1)}, f32[3,256,128]{2,1,0:T(8,128)}, f32[9,256,128]{2,1,0:T(8,128)}) custom-call(bf16[1024,256]{1,0:T(8,128)(2,1)S(1)} %get-tuple-element.8.ig_ref, f32[12,256,128]{2,1,0:T(8,128)S(1)} %get-tuple-element.9.sums_ref), custom_call_target="tpu_custom_call" | custom-call | tf_op jit(solution)/shard_map/pallas_call | solution.py:668
